TPU v7x, 32 devices: a whole 2x2x4 slice. The times are simulated.
32 devices in a mesh: section: 8 (over y, x, core), tensor: 4 (over z).
Axes of the slice: x: 2, y: 2, z: 4, core: 2. Of those that a mesh axis runs over, the one named last changes fastest.
Arguments:
- acts: bfloat16 [8, 2, 32, 4096], P('section', None, None, 'tensor'), may hold values from -6 to 6
- grads_in: bfloat16 [8, 2, 32, 4096], P('section', None, None, 'tensor'), may hold values from -6 to 6
- head_grads: bfloat16 [8, 2, 128, 512], P('section', None, None, 'tensor'), may hold values from -6 to 6
- types: int32 [8, 2, 32], P('section'), may hold values 0 or 1
- gains: bfloat16 [8, 2, 2, 1024], P('section'), may hold values from 0.3984375 to 1.59375
- w_query: bfloat16 [8, 2, 4096, 512], P('section', None, None, 'tensor'), may hold values from -0.09375 to 0.09375
- w_key: bfloat16 [8, 2, 4096, 128], P('section', None, None, 'tensor'), may hold values from -0.09375 to 0.09375
- w_value: bfloat16 [8, 2, 4096, 128], P('section', None, None, 'tensor'), may hold values from -0.09375 to 0.09375
Outputs:
- routed: bfloat16 [8, 2, 32, 4096], P('section', None, None, 'tensor')
All inputs are finite; a program needn't handle non-finite values. No bound on the sum of `types` on one device may be relied on, other than what follows from the above.
Results may differ from a plain program's by a relative error of at most 0.0055.
Values may be sent and summed in bfloat16 or wider, within the bound.
A program may use at most 64 MiB of HBM per device.

v0:
```python
import jax
import jax.numpy as jnp
from jax import lax
from jax.sharding import PartitionSpec as P

HEAD_DIM = 128
SUB = 4


epsilon = 1e-05


def swapped(value, axis, stride):
    mask = 2**stride
    pairs = [(source, source ^ mask) for source in range(lax.axis_size(axis))]
    return lax.ppermute(value, axis, pairs)


def shifted(value, axis, by):
    peers = lax.axis_size(axis)
    return lax.ppermute(value, axis, [(i, (i + by) % peers) for i in range(peers)])


def sum_columns(first, second):
    return (
        lax.psum_scatter(first, "tensor", scatter_dimension=2, tiled=True),
        lax.psum_scatter(second, "tensor", scatter_dimension=2, tiled=True),
    )


def collect_rows(member, position, levels, axis):
    for bit in range(levels):
        partner = swapped(member, "section", bit)
        upper_bit = position >> bit & 1
        member = jnp.where(
            upper_bit == 1,
            jnp.concatenate([partner, member], axis=axis),
            jnp.concatenate([member, partner], axis=axis),
        )
    return member


def halve_once(member, upper_bit, bit):
    half_rows = member.shape[1] // 2
    lower_rows = member[:, :half_rows]
    higher_rows = member[:, half_rows:]
    kept_rows = jnp.where(upper_bit == 1, higher_rows, lower_rows)
    sent_rows = jnp.where(upper_bit == 1, lower_rows, higher_rows)
    return kept_rows + swapped(sent_rows, "section", bit)


def reduce_rows(first, second, position, levels):
    for bit in reversed(range(levels)):
        upper_bit = position >> bit & 1
        first = halve_once(first, upper_bit, bit)
        second = halve_once(second, upper_bit, bit)
    return (first, second)


def per_device(acts, grads_in, head_grads, types, gains, w_query, w_key, w_value):
    tensors = lax.axis_size("tensor")
    section_count = lax.axis_size("section") // SUB
    levels = SUB.bit_length() - 1
    position = lax.axis_index("section") % SUB
    section_here = lax.axis_index("section") // SUB
    x_local = acts[0]
    grad_local = grads_in[0]
    out_grads = head_grads[0]
    w_query = w_query[0]
    w_key = w_key[0]
    w_value = w_value[0]
    x_cols = lax.all_gather(x_local, "tensor", axis=2, tiled=True)
    x_full = collect_rows(x_cols, position, levels, 1)
    kind_full = collect_rows(types[0].astype(jnp.bfloat16), position, levels, 1)
    gain_full = collect_rows(gains[0], position, levels, 2).astype(jnp.float32)
    tokens = x_full.shape[1]
    tokq = x_local.shape[1]
    width = x_full.shape[2]
    cols_dev = x_local.shape[2]
    x_float = x_full.astype(jnp.float32)
    inverse = lax.rsqrt(jnp.mean(x_float * x_float, axis=-1, keepdims=True) + epsilon)
    gain_rows = jnp.where(kind_full[..., None] > 0.5, gain_full[:, 1:2, :], gain_full[:, 0:1, :])
    normed = (x_float * inverse * gain_rows).astype(jnp.bfloat16)
    queries = jnp.einsum(
        "ctd,cdh->cth", normed, w_query, preferred_element_type=jnp.float32
    ).astype(jnp.bfloat16)
    key_part = jnp.einsum("ctd,cdh->cth", normed, w_key, preferred_element_type=jnp.float32).astype(
        jnp.bfloat16
    )
    value_part = jnp.einsum(
        "ctd,cdh->cth", normed, w_value, preferred_element_type=jnp.float32
    ).astype(jnp.bfloat16)
    key_rows, value_rows = (
        lax.all_gather(key_part, "tensor", axis=2, tiled=True),
        lax.all_gather(value_part, "tensor", axis=2, tiled=True),
    )
    softmax_scale = HEAD_DIM ** (-0.5)
    scores = (
        jnp.einsum("cqh,ckh->cqk", queries, key_rows, preferred_element_type=jnp.float32)
        * softmax_scale
    )
    causal = jnp.arange(tokens)[:, None] >= jnp.arange(tokens)[None, :]
    scores = jnp.where(causal[None], scores, -1e30)
    attn_probs = jax.nn.softmax(scores, axis=-1)
    probs_low = attn_probs.astype(jnp.bfloat16)
    prob_grads = jnp.einsum(
        "cqh,ckh->cqk", out_grads, value_rows, preferred_element_type=jnp.float32
    )
    score_grads = (
        attn_probs
        * (prob_grads - jnp.sum(prob_grads * attn_probs, axis=-1, keepdims=True))
        * softmax_scale
    ).astype(jnp.bfloat16)
    query_grads = jnp.einsum(
        "cqk,ckh->cqh", score_grads, key_rows, preferred_element_type=jnp.float32
    ).astype(jnp.bfloat16)
    key_each = jnp.einsum("cqk,cqh->ckh", score_grads, queries, preferred_element_type=jnp.float32)
    value_each = jnp.einsum(
        "cqk,cqh->ckh", probs_low, out_grads, preferred_element_type=jnp.float32
    )
    key_sum, value_sum = sum_columns(key_each, value_each)
    key_grads = key_sum.astype(jnp.bfloat16)
    value_grads = value_sum.astype(jnp.bfloat16)
    joined_grads = jnp.concatenate([query_grads, key_grads, value_grads], axis=2)
    joined_weights = jnp.concatenate([w_query, w_key, w_value], axis=2)
    partial_value = jnp.einsum(
        "cth,cdh->ctd", joined_grads, joined_weights, preferred_element_type=jnp.float32
    )
    stat_part = jnp.sum(x_float * gain_rows * partial_value, axis=-1)
    stat_wide = jnp.broadcast_to(stat_part[..., None], stat_part.shape + (tensors,))
    grad_rows_sum, stat_rows = reduce_rows(partial_value, stat_wide, position, levels)
    grad_mine, stat_mine = sum_columns(grad_rows_sum, stat_rows)
    my_inverse = lax.dynamic_slice_in_dim(inverse, position * tokq, tokq, 1)
    my_gain = lax.dynamic_slice_in_dim(gain_rows, position * tokq, tokq, 1)
    my_gain = lax.dynamic_slice_in_dim(my_gain, lax.axis_index("tensor") * cols_dev, cols_dev, 2)
    my_x = x_local.astype(jnp.float32)
    stat_mean = stat_mine / width
    norm_grads = my_inverse * my_gain * grad_mine - my_x * my_inverse**3 * stat_mean
    result = (grad_local.astype(jnp.float32) + norm_grads).astype(jnp.bfloat16)
    arrived = shifted(result, "section", -SUB)
    routed = jnp.where(section_here == section_count - 1, arrived[::-1], arrived)
    return routed[None]


def solution(mesh):
    return jax.shard_map(
        per_device,
        mesh=mesh,
        in_specs=(
            P("section", None, None, "tensor"),
            P("section", None, None, "tensor"),
            P("section", None, None, "tensor"),
            P("section", None, None),
            P("section", None, None, None),
            P("section", None, None, "tensor"),
            P("section", None, None, "tensor"),
            P("section", None, None, "tensor"),
        ),
        out_specs=P("section", None, None, "tensor"),
        check_vma=False,
    )
```

profile of v0, /device:TPU:0, one launch (start us, length us, event | category | flops | bytes accessed | tf_op | source)
XLA Modules:
  0.0 225.5 jit_solution(11091461946398277763)
XLA Ops:
  7.8 17.7 %all-gather = bf16[1,2,32,4096]{3,2,1,0:T(8,128)(2,1)S(1)} all-gather(bf16[1,2,32,1024]{3,2,1,0:T(8,128)(2,1)} %param.8), channel_id=2, replica_groups=mesh['section'=8,'tensor'=4] {'tensor'}, dimensions={3}, use_global_device_ids=true | all-gather | bytes 655360 | tf_op jit(solution)/shard_map/all_gather | solution.py:72
  25.6 1.5 collective-permute-start.3
  29.2 2.4 %collective-permute-done.5 = bf16[2,2,2048]{2,1,0:T(2,128)(2,1)S(1)} collective-permute-done((bf16[2,2,2048]{2,1,0:T(2,128)(2,1)S(1)}, bf16[2,2,2048]{2,1,0:T(2,128)(2,1)S(1)}, u32[]{:S(2)}, u32[]{:S(2)}) %collective-permute-start.5) | collective-permute-done | bytes 16416 | tf_op jit(solution)/shard_map/ppermute | solution.py:16
  32.7 23.5 %collective-permute-done.1 = bf16[2,64,4096]{2,1,0:T(8,128)(2,1)S(1)} collective-permute-done((bf16[2,64,4096]{2,1,0:T(8,128)(2,1)S(1)}, bf16[2,64,4096]{2,1,0:T(8,128)(2,1)S(1)}, u32[]{:S(2)}, u32[]{:S(2)}) %collective-permute-start.1) | collective-permute-done | bytes 1048608 | tf_op jit(solution)/shard_map/ppermute | solution.py:16
  57.0 1.3 convolution_convert_fusion.2
  58.2 13.4 %all_gather.10 = bf16[2,128,128]{1,2,0:T(8,128)(2,1)S(1)} all-gather(bf16[2,128,32]{1,2,0:T(8,128)(2,1)S(1)} %convolution_convert_fusion.2), channel_id=1, replica_groups=mesh['section'=8,'tensor'=4] {'tensor'}, dimensions={2}, use_global_device_ids=true | all-gather | bytes 81920 | tf_op jit(solution)/shard_map/all_gather | solution.py:94
  71.7 1.3 convolution_convert_fusion.1
  72.9 13.2 %all_gather.11 = bf16[2,128,128]{1,2,0:T(8,128)(2,1)S(1)} all-gather(bf16[2,128,32]{1,2,0:T(8,128)(2,1)S(1)} %convolution_convert_fusion.1), channel_id=1, replica_groups=mesh['section'=8,'tensor'=4] {'tensor'}, dimensions={2}, use_global_device_ids=true | all-gather | bytes 81920 | tf_op jit(solution)/shard_map/all_gather | solution.py:95
  86.2 1.4 fusion.22
  89.6 1.9 fusion.25
  91.6 2.8 %copy.11 = bf16[1,2,4096,128]{2,3,1,0:T(8,128)(2,1)} copy(bf16[1,2,4096,128]{3,2,1,0:T(8,128)(2,1)S(1)} %copy-done.1) | data formatting | bytes 4194304 | tf_op args[5]
  95.6 13.9 %reduce-scatter.6.cloned.1.call-done = f32[2,128,32]{1,2,0:T(8,128)} async-done(((f32[2,128,128]{1,2,0:T(8,128)}), f32[2,128,32]{1,2,0:T(8,128)}) %reduce-scatter.6.cloned.1.call-update) | async-done | bytes 32784 | tf_op jit(solution)/shard_map/reduce_scatter | solution.py:27
  110.2 19.1 %reduce-scatter.4.cloned.1.call-done = f32[2,128,32]{1,2,0:T(8,128)} async-done(((f32[2,128,128]{1,2,0:T(8,128)}), f32[2,128,32]{1,2,0:T(8,128)}) %reduce-scatter.4.cloned.1.call-update) | async-done | bytes 32784 | tf_op jit(solution)/shard_map/reduce_scatter | solution.py:26
  130.1 5.5 %fusion.6 = (f32[2,128]{1,0:T(2,128)S(1)}, f32[2,128,4096]{2,1,0:T(8,128)}, f32[2,128,4096]{2,1,0:T(8,128)S(1)}) fusion(f32[2,4096]{1,0:T(2,128)S(1)} %copy-done.6, f32[2,4096]{1,0:T(2,128)S(1)} %copy-done.8, pred[2,128]{1,0:T(4,128)(4,1)} %copy-done.11, bf16[2,64,4096]{2,1,0:T(8,128)(2,1)} %copy-done.2, bf16[2,64,4096]{2,1,0:T(8,128)(2,1)S(1)} %maximum_select_fusion.1, ...), kind=kOutput, calls=%fused_computation.9 | convolution fusion | flops 427065088 | bytes 13796609 | tf_op jit(solution)/shard_map/cth,cdh->ctd/dot_general | solution.py:126
  135.9 1.5 collective-permute-start.6
  137.5 43.5 %collective-permute-done.6 = f32[2,64,4096]{2,1,0:T(8,128)S(1)} collective-permute-done((f32[2,64,4096]{2,1,0:T(8,128)S(1)}, f32[2,64,4096]{2,1,0:T(8,128)S(1)}, u32[]{:S(2)}, u32[]{:S(2)}) %collective-permute-start.6) | collective-permute-done | bytes 2097184 | tf_op jit(solution)/shard_map/ppermute | solution.py:16
  181.7 2.6 %collective-permute-done.7 = f32[2,32,4096]{2,1,0:T(8,128)S(1)} collective-permute-done((f32[2,32,4096]{2,1,0:T(8,128)S(1)}, f32[2,32,4096]{2,1,0:T(8,128)S(1)}, u32[]{:S(2)}, u32[]{:S(2)}) %collective-permute-start.7) | collective-permute-done | bytes 1048608 | tf_op jit(solution)/shard_map/ppermute | solution.py:16
  185.6 1.5 collective-permute-start.8
  187.7 1.6 collective-permute-done.8
  190.6 10.0 %all-reduce = f32[2,32,4]{1,0,2:T(2,128)S(1)} all-reduce(f32[2,32,4]{1,0,2:T(2,128)S(1)} %select_add_fusion.2), channel_id=6, replica_groups=mesh['section'=8,'tensor'=4] {'tensor'}, use_global_device_ids=true, to_apply=%region_8.9.clone | all-reduce | flops 256 | bytes 2048
  201.2 10.7 %reduce-scatter.8.cloned.1.call-done = f32[2,32,1024]{2,1,0:T(8,128)} async-done(((f32[2,32,4096]{2,1,0:T(8,128)}), f32[2,32,1024]{2,1,0:T(8,128)}) %reduce-scatter.8.cloned.1.call-update) | async-done | bytes 262160 | tf_op jit(solution)/shard_map/reduce_scatter | solution.py:26
  212.0 1.2 fusion.32
  213.2 1.5 collective-permute-start.10
  214.8 3.5 %collective-permute-done.10 = bf16[2,32,1024]{2,1,0:T(8,128)(2,1)S(1)} collective-permute-done((bf16[2,32,1024]{2,1,0:T(8,128)(2,1)S(1)}, bf16[2,32,1024]{2,1,0:T(8,128)(2,1)S(1)}, u32[]{:S(2)}, u32[]{:S(2)}) %collective-permute-start.10) | collective-permute-done | bytes 131104 | tf_op jit(solution)/shard_map/ppermute | solution.py:21
  (80 shorter events, 15.5 us)
Async XLA Ops:
  6.5 81.9 %copy-start = (bf16[1,2,128,128]{3,2,1,0:T(8,128)(2,1)S(1)}, bf16[1,2,128,128]{3,2,1,0:T(8,128)(2,1)}, u32[]{:S(2)}) copy-start(bf16[1,2,128,128]{3,2,1,0:T(8,128)(2,1)} %param.10) | copy-start | bytes 196612
  6.5 50.4 %copy-start.12 = (bf16[1,2,4096,32]{2,3,1,0:T(8,128)(2,1)S(1)}, bf16[1,2,4096,32]{2,3,1,0:T(8,128)(2,1)}, u32[]{:S(2)}) copy-start(bf16[1,2,4096,32]{2,3,1,0:T(8,128)(2,1)} %param.14) | copy-start | bytes 1572868
  6.5 102.9 %reduce-scatter.6.cloned.1.call-start = ((), (), s32[]{:S(2)}) async-start(), calls=%async_computation.4 | async-start | bytes 163840 | tf_op jit(solution)/shard_map/reduce_scatter | solution.py:27
  7.3 18.2 %collective-permute-start.2 = (bf16[2,32]{1,0:T(2,128)(2,1)S(1)}, bf16[2,32]{1,0:T(2,128)(2,1)S(1)}, u32[]{:S(2)}, u32[]{:S(2)}) collective-permute-start(bf16[2,32]{1,0:T(2,128)(2,1)S(1)} %convert_bitcast_fusion), channel_id=1, source_target_pairs={{0,4},{4,0},{8,12},{12,8},{16,20},{20,16},{24,28},{28,24},{1,5},{5... | collective-permute-start | bytes 392 | tf_op jit(solution)/shard_map/ppermute | solution.py:16
  7.8 19.3 %collective-permute-start.4 = (bf16[2,2,1024]{2,1,0:T(2,128)(2,1)}, bf16[2,2,1024]{2,1,0:T(2,128)(2,1)S(1)}, u32[]{:S(2)}, u32[]{:S(2)}) collective-permute-start(bf16[2,2,1024]{2,1,0:T(2,128)(2,1)} %bitcast.58), channel_id=1, source_target_pairs={{0,4},{4,0},{8,12},{12,8},{16,20},{20,16},{24,28},{28,24},{1,5},{5... | collective-permute-start | bytes 24584 | tf_op jit(solution)/shard_map/ppermute | solution.py:16
  25.5 6.3 %collective-permute-start = (bf16[2,32,4096]{2,1,0:T(8,128)(2,1)S(1)}, bf16[2,32,4096]{2,1,0:T(8,128)(2,1)S(1)}, u32[]{:S(2)}, u32[]{:S(2)}) collective-permute-start(bf16[2,32,4096]{2,1,0:T(8,128)(2,1)S(1)} %bitcast.52), channel_id=1, source_target_pairs={{0,4},{4,0},{8,12},{12,8},{16,20},{20,16},{24,28},{28,24},{1,5},{5... | collective-permute-start | bytes 1572872 | tf_op jit(solution)/shard_map/ppermute | solution.py:16
  25.6 3.6 %collective-permute-start.3 = (bf16[2,64]{1,0:T(2,128)(2,1)S(1)}, bf16[2,64]{1,0:T(2,128)(2,1)S(1)}, u32[]{:S(2)}, u32[]{:S(2)}) collective-permute-start(bf16[2,64]{1,0:T(2,128)(2,1)S(1)} %broadcast_select_fusion.6), channel_id=1, source_target_pairs={{0,8},{4,12},{8,0},{12,4},{16,24},{20,28},{24,16},{28,20},{1,9},{5... | collective-permute-start | bytes 776 | tf_op jit(solution)/shard_map/ppermute | solution.py:16
  27.9 3.8 %collective-permute-start.5 = (bf16[2,2,2048]{2,1,0:T(2,128)(2,1)S(1)}, bf16[2,2,2048]{2,1,0:T(2,128)(2,1)S(1)}, u32[]{:S(2)}, u32[]{:S(2)}) collective-permute-start(bf16[2,2,2048]{2,1,0:T(2,128)(2,1)S(1)} %broadcast_select_fusion.2), channel_id=1, source_target_pairs={{0,8},{4,12},{8,0},{12,4},{16,24},{20,28},{24,16},{28,20},{1,9},{5... | collective-permute-start | bytes 49160 | tf_op jit(solution)/shard_map/ppermute | solution.py:16
  29.2 56.9 %copy-start.11 = (pred[2,128]{1,0:T(4,128)(4,1)}, pred[2,128]{1,0:T(4,128)(4,1)S(1)}, u32[]{:S(2)}) copy-start(pred[2,128]{1,0:T(4,128)(4,1)S(1)} %fusion.52) | copy-start | bytes 772
  32.0 24.2 %collective-permute-start.1 = (bf16[2,64,4096]{2,1,0:T(8,128)(2,1)S(1)}, bf16[2,64,4096]{2,1,0:T(8,128)(2,1)S(1)}, u32[]{:S(2)}, u32[]{:S(2)}) collective-permute-start(bf16[2,64,4096]{2,1,0:T(8,128)(2,1)S(1)} %maximum_select_fusion.1), channel_id=1, source_target_pairs={{0,8},{4,12},{8,0},{12,4},{16,24},{20,28},{24,16},{28,20},{1,9},{5... | collective-permute-start | bytes 3145736 | tf_op jit(solution)/shard_map/ppermute | solution.py:16
  32.7 53.5 %copy-start.5 = (f32[2,4096]{1,0:T(2,128)}, f32[2,4096]{1,0:T(2,128)S(1)}, u32[]{:S(2)}) copy-start(f32[2,4096]{1,0:T(2,128)S(1)} %get-tuple-element.16) | copy-start | bytes 98308
  32.7 53.5 %copy-start.7 = (f32[2,4096]{1,0:T(2,128)}, f32[2,4096]{1,0:T(2,128)S(1)}, u32[]{:S(2)}) copy-start(f32[2,4096]{1,0:T(2,128)S(1)} %get-tuple-element.17) | copy-start | bytes 98308
  56.2 30.0 %copy-start.2 = (bf16[2,64,4096]{2,1,0:T(8,128)(2,1)}, bf16[2,64,4096]{2,1,0:T(8,128)(2,1)S(1)}, u32[]{:S(2)}) copy-start(bf16[2,64,4096]{2,1,0:T(8,128)(2,1)S(1)} %collective-permute-done.1) | copy-start | bytes 3145732
  89.4 40.0 %reduce-scatter.4.cloned.1.call-start = ((), (), s32[]{:S(2)}) async-start(), calls=%async_computation.3 | async-start | bytes 163840 | tf_op jit(solution)/shard_map/reduce_scatter | solution.py:26
  89.6 40.5 %copy-start.6 = (f32[2,4096]{1,0:T(2,128)S(1)}, f32[2,4096]{1,0:T(2,128)}, u32[]{:S(2)}) copy-start(f32[2,4096]{1,0:T(2,128)} %copy-done.5) | copy-start | bytes 98308
  89.6 40.5 %copy-start.8 = (f32[2,4096]{1,0:T(2,128)S(1)}, f32[2,4096]{1,0:T(2,128)}, u32[]{:S(2)}) copy-start(f32[2,4096]{1,0:T(2,128)} %copy-done.7) | copy-start | bytes 98308
  91.5 120.5 %reduce-scatter.8.cloned.1.call-start = ((), (), s32[]{:S(2)}) async-start(), calls=%async_computation.5 | async-start | bytes 1310720 | tf_op jit(solution)/shard_map/reduce_scatter | solution.py:26
  135.9 45.1 %collective-permute-start.6 = (f32[2,64,4096]{2,1,0:T(8,128)S(1)}, f32[2,64,4096]{2,1,0:T(8,128)S(1)}, u32[]{:S(2)}, u32[]{:S(2)}) collective-permute-start(f32[2,64,4096]{2,1,0:T(8,128)S(1)} %slice_select_fusion), channel_id=1, source_target_pairs={{0,8},{4,12},{8,0},{12,4},{16,24},{20,28},{24,16},{28,20},{1,9},{5... | collective-permute-start | bytes 6291464 | tf_op jit(solution)/shard_map/ppermute | solution.py:16
  181.6 30.4 %copy-start.3 = (bf16[1,2,32,1024]{3,2,1,0:T(8,128)(2,1)S(1)}, bf16[1,2,32,1024]{3,2,1,0:T(8,128)(2,1)}, u32[]{:S(2)}) copy-start(bf16[1,2,32,1024]{3,2,1,0:T(8,128)(2,1)} %param.8) | copy-start | bytes 393220
  181.6 30.4 %copy-start.4 = (bf16[1,2,32,1024]{3,2,1,0:T(8,128)(2,1)S(1)}, bf16[1,2,32,1024]{3,2,1,0:T(8,128)(2,1)}, u32[]{:S(2)}) copy-start(bf16[1,2,32,1024]{3,2,1,0:T(8,128)(2,1)} %param.9) | copy-start | bytes 393220
  181.6 2.7 %collective-permute-start.7 = (f32[2,32,4096]{2,1,0:T(8,128)S(1)}, f32[2,32,4096]{2,1,0:T(8,128)S(1)}, u32[]{:S(2)}, u32[]{:S(2)}) collective-permute-start(f32[2,32,4096]{2,1,0:T(8,128)S(1)} %slice_select_fusion.1), channel_id=1, source_target_pairs={{0,4},{4,0},{8,12},{12,8},{16,20},{20,16},{24,28},{28,24},{1,5},{5... | collective-permute-start | bytes 3145736 | tf_op jit(solution)/shard_map/ppermute | solution.py:16
  185.6 3.6 %collective-permute-start.8 = (f32[2,64,4]{1,0,2:T(2,128)S(1)}, f32[2,64,4]{1,0,2:T(2,128)S(1)}, u32[]{:S(2)}, u32[]{:S(2)}) collective-permute-start(f32[2,64,4]{1,0,2:T(2,128)S(1)} %broadcast_in_dim.67), channel_id=1, source_target_pairs={{0,8},{4,12},{8,0},{12,4},{16,24},{20,28},{24,16},{28,20},{1,9},{5... | collective-permute-start | bytes 6152 | tf_op jit(solution)/shard_map/ppermute | solution.py:16
  189.3 1.2 collective-permute-start.9
  213.2 5.0 %collective-permute-start.10 = (bf16[2,32,1024]{2,1,0:T(8,128)(2,1)S(1)}, bf16[2,32,1024]{2,1,0:T(8,128)(2,1)S(1)}, u32[]{:S(2)}, u32[]{:S(2)}) collective-permute-start(bf16[2,32,1024]{2,1,0:T(8,128)(2,1)S(1)} %fusion.32), channel_id=1, source_target_pairs={{0,16},{4,20},{8,24},{12,28},{16,0},{20,4},{24,8},{28,12},{1,17},{... | collective-permute-start | bytes 393224 | tf_op jit(solution)/shard_map/ppermute | solution.py:21
  (5 other events, 71.8 us)
Sparse Core Ops, SparseCore 0:
  89.5 19.9 reduce-scatter.5
  111.7 17.5 reduce-scatter.3
  185.7 26.2 reduce-scatter.7
where the time goes:
time: 226 us; the launch traced here: 225 us
  waiting for transfers between devices  123 us (54%)
  blocking collectives  54.3 us (24%)
  matrix products  13.8 us (6%)
  between operations  13.4 us (6%)
  other arithmetic  9.83 us (4%)
  starting transfers between devices  7.91 us (4%)
  local copies, waits for them, and re-layouts  3.58 us (2%)
    ppermute x10, waiting for transfers between devices, swapped(): return lax.ppermute(value, axis, pairs)  75.4 us
    reduce_scatter x2, waiting for transfers between devices, sum_columns(): lax.psum_scatter(first, 'tensor', scatter_dimension=2, tiled=True)  29.9 us
    all_gather x1, blocking collectives, per_device(): x_cols = lax.all_gather(x_local, 'tensor', axis=2, tiled=True)  17.7 us
    reduce_scatter x1, waiting for transfers between devices, sum_columns(): lax.psum_scatter(second, 'tensor', scatter_dimension=2, tiled=True)  13.9 us
    all_gather x1, blocking collectives, per_device(): lax.all_gather(key_part, 'tensor', axis=2, tiled=True)  13.4 us
    all_gather x1, blocking collectives, per_device(): lax.all_gather(value_part, 'tensor', axis=2, tiled=True)  13.2 us
    unnamed x1, blocking collectives  10 us
    ppermute x10, starting transfers between devices, swapped(): return lax.ppermute(value, axis, pairs)  6.29 us
  transfers between devices with their start and end apart: 14, of which 11 were waited for; matrix products, arithmetic and copies ran while one was open for 4% of the time, Pallas kernels for 0%

commit v1 on v0

v1 whole, which is shorter than its diff:
```python
import jax
import jax.numpy as jnp
from jax import lax
from jax.experimental import pallas as pl
from jax.experimental.pallas import tpu as pltpu
from jax.sharding import PartitionSpec as P

SUB = 4
EPS = 1e-05
MESH = pl.DeviceIdType.MESH
F32 = jnp.float32
BF16 = jnp.bfloat16
LEFT, RIGHT, ACROSS, PAIR = 0, 1, 2, 3


def dot(a, b, dims):
    return lax.dot_general(a, b, (dims, ((), ())), preferred_element_type=F32)


def kernel(
    sections, tensors,
    acts, grads, heads, types, gains, wq, wk, wv,
    out,
    xg, kinds, gain_all, wqv, wkv, wvv, wcat, hg, gr, kindc, invc,
    kvt, dkv, dkv_in, stat, stat_z, stat_s, stat_in,
    part, part_in, xs, xr, zs0, zr0, zs1, zr1, xs1, xr1, res,
    loc, ag_s, ag_r, small_s, small_r, kv_s, kv_r, dk_s, dk_r, st_s, st_r, sp_s, sp_r,
    pair_s, pair_r, x_s, x_r, z_s, z_r, route_s, route_r,
):
    spans, rows, cols = acts.shape
    n = SUB * rows
    hd = wq.shape[2]
    kc = wk.shape[2]
    width = cols * tensors
    gcols = gains.shape[2]
    T = tensors
    t = lax.axis_index("tensor")
    sec = lax.axis_index("section")
    pos = lax.rem(sec, SUB)
    here = sec // SUB
    base = here * SUB
    xi = pos // 2
    ci = lax.rem(pos, 2)
    pos_pair = xi * 2 + (1 - ci)
    pos_x = (1 - xi) * 2 + ci
    pair_dev = (base + pos_pair, t)
    x_dev = (base + pos_x, t)
    left_dev = (sec, lax.max(t - 1, 0))
    right_dev = (sec, lax.min(t + 1, T - 1))
    before = lax.rem(here + sections - 1, sections) * SUB + pos
    after = lax.rem(here + 1, sections) * SUB + pos

    def pos_peer(k):
        return (base + lax.rem(pos + k, SUB), t)

    def z_peer(k):
        return (sec, lax.rem(t + k, T))

    def send(src, dst, ssem, rsem, dev):
        pltpu.make_async_remote_copy(
            src_ref=src, dst_ref=dst, send_sem=ssem, recv_sem=rsem, device_id=dev, device_id_type=MESH
        ).start()

    def sent(src, ssem):
        pltpu.make_async_copy(src, src, ssem).wait()

    def arrived(dst, rsem):
        pltpu.make_async_copy(dst, dst, rsem).wait()

    def rowpos(p):
        return pl.ds(pl.multiple_of(p * rows, rows), rows)

    def blk(v, p, tt):
        return xg.at[v, rowpos(p), pl.ds(pl.multiple_of(tt * cols, cols), cols)]

    own = [pltpu.make_async_copy(acts.at[v], blk(v, pos, t), loc.at[v]) for v in range(2)]
    kload = pltpu.make_async_copy(types, kinds.at[pos], loc.at[2])
    gload = pltpu.make_async_copy(gains, gain_all.at[pos], loc.at[3])
    wload = [
        pltpu.make_async_copy(wq, wqv, loc.at[4]),
        pltpu.make_async_copy(wk, wkv, loc.at[5]),
        pltpu.make_async_copy(wv, wvv, loc.at[6]),
    ]
    hload = pltpu.make_async_copy(heads, hg, loc.at[7])
    grload = pltpu.make_async_copy(grads, gr, loc.at[8])
    for copy in own + [kload, gload] + wload + [hload, grload]:
        copy.start()

    barrier = pltpu.get_barrier_semaphore()
    greeted = [pos_peer(k) for k in range(1, SUB)] + [z_peer(k) for k in range(1, T)]
    greeted += [(before, t), (after, t)]
    for dev in greeted:
        pl.semaphore_signal(barrier, inc=1, device_id=dev, device_id_type=MESH)
    pl.semaphore_wait(barrier, len(greeted))

    def ag_send(kind, v, p, tt):
        dev = (left_dev, right_dev, x_dev, pair_dev)[kind]
        send(blk(v, p, tt), blk(v, p, tt), ag_s.at[v, kind, p, tt], ag_r.at[v, p, tt], dev)

    def ag_wait(v, p, tt):
        arrived(blk(v, p, tt), ag_r.at[v, p, tt])

    def ag_sides(v, p, tt):
        @pl.when(t > 0)
        def _():
            ag_send(LEFT, v, p, tt)

        @pl.when(t < T - 1)
        def _():
            ag_send(RIGHT, v, p, tt)

    own[0].wait()
    ag_send(ACROSS, 0, pos, t)
    own[1].wait()
    ag_sides(1, pos, t)
    ag_sides(0, pos, t)
    ag_send(ACROSS, 1, pos, t)
    ag_send(PAIR, 0, pos, t)
    ag_send(PAIR, 1, pos, t)
    kload.wait()
    gload.wait()
    for k in range(1, SUB):
        send(kinds.at[pos], kinds.at[pos], small_s.at[0, k], small_r.at[0, k], pos_peer(k))
        send(gain_all.at[pos], gain_all.at[pos], small_s.at[1, k], small_r.at[1, k], pos_peer(k))

    for copy in wload:
        copy.wait()

    def join_weights(v):
        for i in range(T):
            at = pl.ds(i * cols, cols)
            wcat[v, at, :hd] = wqv[v, at, :]
            wcat[v, at, hd:] = jnp.concatenate([wkv[v, at, :], wvv[v, at, :]], axis=1)

    join_weights(0)

    ag_wait(0, pos_x, t)
    ag_sides(0, pos_x, t)
    ag_send(PAIR, 0, pos_x, t)

    for k in range(1, T):
        for low in (True, False):
            tt = t - k if low else t + k
            ok = tt >= 0 if low else tt < T
            onward = t < T - 1 if low else t > 0
            kind = RIGHT if low else LEFT

            @pl.when(ok)
            def _():
                ag_wait(1, pos, tt)

                @pl.when(onward)
                def _():
                    ag_send(kind, 1, pos, tt)

                ag_send(ACROSS, 1, pos, tt)
                ag_send(PAIR, 1, pos, tt)
                for p in (pos, pos_x):
                    ag_wait(0, p, tt)

                    @pl.when(onward)
                    def _():
                        ag_send(kind, 0, p, tt)

                    ag_send(PAIR, 0, p, tt)

        if k == 1:
            join_weights(1)
            ag_wait(1, pos_x, t)
            ag_send(PAIR, 1, pos_x, t)
    for k in range(1, T):
        for low in (True, False):
            tt = t - k if low else t + k
            ok = tt >= 0 if low else tt < T

            @pl.when(ok)
            def _():
                ag_wait(1, pos_x, tt)
                ag_send(PAIR, 1, pos_x, tt)

    for k in range(1, SUB):
        source = lax.rem(pos - k + SUB, SUB)
        arrived(kinds.at[source], small_r.at[0, k])
        arrived(gain_all.at[source], small_r.at[1, k])
    eye_r = lax.broadcasted_iota(jnp.int32, (rows, rows), 0) == lax.broadcasted_iota(
        jnp.int32, (rows, rows), 1
    )
    for v in range(2):
        for p in range(SUB):
            line = kinds[p, v : v + 1, :].astype(F32)
            column = jnp.sum(jnp.where(eye_r, line, 0.0), axis=1, keepdims=True)
            kindc[v, p * rows : (p + 1) * rows, :] = jnp.broadcast_to(column, (rows, 128))

    for v in range(2):
        for p in (pos_pair, (1 - xi) * 2 + (1 - ci)):
            for tt in range(T):
                ag_wait(v, p, tt)

    hload.wait()
    eye = lax.broadcasted_iota(jnp.int32, (n, n), 0) == lax.broadcasted_iota(jnp.int32, (n, n), 1)
    queries = []
    for v in range(2):
        speech = kindc[v, :, 0:1] > 0.5
        total = jnp.zeros((n, hd + 2 * kc), F32)
        square = jnp.zeros((n, 1), F32)
        for i in range(T):
            at = pl.ds(i * cols, cols)
            block = i * cols // gcols
            off = i * cols % gcols
            pair = gain_all[block, v, :, off : off + cols].astype(F32)
            xf = xg[v, :, at].astype(F32)
            square = square + jnp.sum(xf * xf, axis=1, keepdims=True)
            scaled = (xf * jnp.where(speech, pair[1:2, :], pair[0:1, :])).astype(BF16)
            total = total + dot(scaled, wcat[v, at, :], ((1,), (0,)))
        inverse = lax.rsqrt(square / width + EPS)
        invc[v] = jnp.broadcast_to(inverse, (n, 128))
        total = total * inverse
        queries.append(total[:, :hd].astype(BF16))
        turned = jnp.transpose(total[:, hd:]).astype(BF16)
        mine = pl.ds(pl.multiple_of(t * kc, kc), kc)
        kvt[v, 0, mine, :] = turned[:kc]
        kvt[v, 1, mine, :] = turned[kc:]
    mine = pl.ds(pl.multiple_of(t * kc, kc), kc)
    for k in range(1, T):
        send(kvt.at[:, :, mine, :], kvt.at[:, :, mine, :], kv_s.at[k], kv_r.at[k], z_peer(k))
    for k in range(1, T):
        source = lax.rem(t - k + T, T)
        theirs = kvt.at[:, :, pl.ds(pl.multiple_of(source * kc, kc), kc), :]
        arrived(theirs, kv_r.at[k])

    scale = hd ** (-0.5)
    causal = lax.broadcasted_iota(jnp.int32, (n, n), 0) >= lax.broadcasted_iota(
        jnp.int32, (n, n), 1
    )
    query_grads = []
    for v in range(2):
        kt = kvt[v, 0]
        vt = kvt[v, 1]
        og = hg[v]
        scores = dot(queries[v], kt, ((1,), (0,))) * scale
        scores = jnp.where(causal, scores, -1e30)
        top = jnp.max(scores, axis=1, keepdims=True)
        weights = jnp.exp(scores - top)
        probs = weights / jnp.sum(weights, axis=1, keepdims=True)
        pg = dot(og, vt, ((1,), (0,)))
        sg = probs * (pg - jnp.sum(pg * probs, axis=1, keepdims=True)) * scale
        sg = sg.astype(BF16)
        key_each = dot(queries[v], sg, ((0,), (0,)))
        value_each = dot(og, probs.astype(BF16), ((0,), (0,)))
        dkv[v, 0] = key_each.astype(BF16)
        dkv[v, 1] = value_each.astype(BF16)
        qg = dot(sg, kt, ((1,), (1,)))
        query_grads.append(qg.astype(BF16))
        column = jnp.sum(qg * queries[v].astype(F32), axis=1, keepdims=True)
        line = jnp.sum(jnp.where(eye, column, 0.0), axis=0, keepdims=True)
        line = line + jnp.sum(
            key_each * kt.astype(F32) + value_each * vt.astype(F32), axis=0, keepdims=True
        )
        stat[v] = jnp.broadcast_to(line, (8, n))
    for k in range(1, T):
        goal = pl.ds(pl.multiple_of(lax.rem(t + k, T) * kc, kc), kc)
        send(dkv.at[:, :, goal, :], dkv_in.at[k - 1], dk_s.at[k], dk_r.at[k], z_peer(k))
        send(stat, stat_z.at[k - 1], st_s.at[k], st_r.at[k], z_peer(k))
    summed = dkv[:, :, mine, :].astype(F32)
    for k in range(1, T):
        arrived(dkv_in.at[k - 1], dk_r.at[k])
        summed = summed + dkv_in[k - 1].astype(F32)

    for v in range(2):
        kv_rows = jnp.transpose(summed[v].reshape(2 * kc, n)).astype(BF16)
        joined = jnp.concatenate([query_grads[v], kv_rows], axis=1)
        for i in range(T):
            piece = dot(joined, wcat[v, pl.ds(i * cols, cols), :], ((1,), (1,))).astype(BF16)
            for p in range(SUB):
                part[v, p // 2, p % 2, i] = piece[p * rows : (p + 1) * rows]
            send(part.at[v, :, 1 - ci, i], part_in.at[v, :, i], pair_s.at[v, i], pair_r.at[v, i], pair_dev)

    line = stat[...]
    for k in range(1, T):
        arrived(stat_z.at[k - 1], st_r.at[k])
        line = line + stat_z[k - 1]
    stat_s[...] = line
    for k in range(1, SUB):
        send(stat_s, stat_in.at[k - 1], sp_s.at[k], sp_r.at[k], pos_peer(k))

    for i in range(T):
        arrived(part_in.at[0, :, i], pair_r.at[0, i])
        xs[i] = (part[0, 1 - xi, ci, i].astype(F32) + part_in[0, 1 - xi, i].astype(F32)).astype(BF16)
        send(xs.at[i], xr.at[i], x_s.at[i], x_r.at[i], x_dev)
    for i in range(T):
        arrived(part_in.at[1, :, i], pair_r.at[1, i])

    def held0(i):
        return (
            part[0, xi, ci, i].astype(F32) + part_in[0, xi, i].astype(F32) + xr[i].astype(F32)
        )

    def held1(i):
        return part[1, :, ci, i].astype(F32) + part_in[1, :, i].astype(F32)

    bufs = ((zs0, zr0, held0), (zs1, zr1, held1))

    def step(v, goal, right):
        stage, landing, held = bufs[v]
        side = 0 if right else 1
        first = t == 0 if right else t == T - 1
        dev = right_dev if right else left_dev

        @pl.when(first)
        def _():
            stage[goal] = held(goal).astype(BF16)

        @pl.when(jnp.logical_not(first))
        def _():
            arrived(landing.at[side, goal], z_r.at[v, side, goal])
            stage[goal] = (held(goal) + landing[side, goal].astype(F32)).astype(BF16)

        send(stage.at[goal], landing.at[side, goal], z_s.at[v, goal], z_r.at[v, side, goal], dev)

    for i in range(T - 1):
        for v in (1, 0):
            if v == 0 and i == 0:
                for j in range(T):
                    arrived(xr.at[j], x_r.at[j])
            high = T - 1 - i

            @pl.when(t < high)
            def _():
                step(v, high, True)

            @pl.when(t > i)
            def _():
                step(v, i, False)

    def settle(v):
        stage, landing, held = bufs[v]
        stage[t] = held(t).astype(BF16)

        @pl.when(t > 0)
        def _():
            arrived(landing.at[0, t], z_r.at[v, 0, t])
            stage[t] = (stage[t].astype(F32) + landing[0, t].astype(F32)).astype(BF16)

        @pl.when(t < T - 1)
        def _():
            arrived(landing.at[1, t], z_r.at[v, 1, t])
            stage[t] = (stage[t].astype(F32) + landing[1, t].astype(F32)).astype(BF16)

    settle(1)
    xs1[...] = zs1[t, 1 - xi]
    send(xs1, xr1, x_s.at[T], x_r.at[T], x_dev)
    settle(0)

    grload.wait()
    line = stat_s[...]
    for k in range(1, SUB):
        arrived(stat_in.at[k - 1], sp_r.at[k])
        line = line + stat_in[k - 1]
    lane = lax.broadcasted_iota(jnp.int32, (rows, n), 1)
    row = lax.broadcasted_iota(jnp.int32, (rows, n), 0)
    pick = lane == row + pos * rows
    gain_block = t * cols // gcols
    gain_off = pl.multiple_of(lax.rem(t * cols, gcols), cols)

    def finish(v, grad_sum):
        mean = jnp.sum(jnp.where(pick, line[v, 0:1, :], 0.0), axis=1, keepdims=True) / width
        inverse = invc[v, rowpos(pos), 0:1]
        speech = kindc[v, rowpos(pos), 0:1] > 0.5
        pair = gain_all[gain_block, v, :, pl.ds(gain_off, cols)].astype(F32)
        gain = jnp.where(speech, pair[1:2, :], pair[0:1, :])
        x = xg[v, rowpos(pos), pl.ds(pl.multiple_of(t * cols, cols), cols)].astype(F32)
        res[v] = (
            gr[v].astype(F32) + inverse * gain * grad_sum - x * (inverse * inverse * mean)
        ).astype(BF16)
        goal = jnp.where(here == 0, 1 - v, v)
        send(res.at[v], out.at[goal], route_s.at[v], route_r.at[goal], (before, t))

    finish(0, zs0[t].astype(F32))
    arrived(xr1, x_r.at[T])
    finish(1, zs1[t, xi].astype(F32) + xr1[...].astype(F32))

    for v in range(2):
        for kind in (LEFT, RIGHT):
            edge = t > 0 if kind == LEFT else t < T - 1
            for tt in range(T):
                use = jnp.logical_and(edge, tt >= t if kind == LEFT else tt <= t)
                for p in (pos, pos_x):
                    if v == 1 and p is pos_x:
                        continue

                    @pl.when(use)
                    def _():
                        sent(blk(v, p, tt), ag_s.at[v, kind, p, tt])

        for tt in range(T):
            for p in (pos, pos_x):
                sent(blk(v, p, tt), ag_s.at[v, PAIR, p, tt])
            if v == 1:
                sent(blk(v, pos, tt), ag_s.at[v, ACROSS, pos, tt])
    sent(blk(0, pos, t), ag_s.at[0, ACROSS, pos, t])
    for k in range(1, SUB):
        sent(kinds.at[pos], small_s.at[0, k])
        sent(gain_all.at[pos], small_s.at[1, k])
        sent(stat_s, sp_s.at[k])
    for k in range(1, T):
        sent(kvt.at[:, :, mine, :], kv_s.at[k])
        goal = pl.ds(pl.multiple_of(lax.rem(t + k, T) * kc, kc), kc)
        sent(dkv.at[:, :, goal, :], dk_s.at[k])
        sent(stat, st_s.at[k])
    for v in range(2):
        for i in range(T):
            sent(part.at[v, :, 1 - ci, i], pair_s.at[v, i])

            @pl.when(i != t)
            def _():
                sent(bufs[v][0].at[i], z_s.at[v, i])
    for i in range(T):
        sent(xs.at[i], x_s.at[i])
    sent(xs1, x_s.at[T])
    for v in range(2):
        sent(res.at[v], route_s.at[v])
        arrived(out.at[v], route_r.at[v])


def per_device(sections, acts, grads_in, head_grads, types, gains, w_query, w_key, w_value):
    T = lax.axis_size("tensor")
    acts, grads_in, head_grads, types, gains = acts[0], grads_in[0], head_grads[0], types[0], gains[0]
    w_query, w_key, w_value = w_query[0], w_key[0], w_value[0]
    spans, rows, cols = acts.shape
    n = SUB * rows
    hd = w_query.shape[2]
    kc = w_key.shape[2]
    width = cols * T
    V = pltpu.VMEM
    D = pltpu.SemaphoreType.DMA
    scratch = [
        V((2, n, width), BF16), V((SUB, 2, rows), jnp.int32), V((SUB,) + gains.shape, BF16),
        V(w_query.shape, BF16), V(w_key.shape, BF16), V(w_value.shape, BF16),
        V((2, width, hd + 2 * kc), BF16), V(head_grads.shape, BF16), V(grads_in.shape, BF16),
        V((2, n, 128), F32), V((2, n, 128), F32),
        V((2, 2, hd, n), BF16), V((2, 2, hd, n), BF16), V((T - 1, 2, 2, kc, n), BF16),
        V((2, 8, n), F32), V((T - 1, 2, 8, n), F32), V((2, 8, n), F32), V((SUB - 1, 2, 8, n), F32),
        V((2, 2, 2, T, rows, cols), BF16), V((2, 2, T, rows, cols), BF16),
        V((T, rows, cols), BF16), V((T, rows, cols), BF16),
        V((T, rows, cols), BF16), V((2, T, rows, cols), BF16),
        V((T, 2, rows, cols), BF16), V((2, T, 2, rows, cols), BF16),
        V((rows, cols), BF16), V((rows, cols), BF16), V((2, rows, cols), BF16),
        D((9,)), D((2, 4, SUB, T)), D((2, SUB, T)), D((2, SUB)), D((2, SUB)),
        D((T,)), D((T,)), D((T,)), D((T,)), D((T,)), D((T,)), D((SUB,)), D((SUB,)),
        D((2, T)), D((2, T)), D((T + 1,)), D((T + 1,)), D((2, T)), D((2, 2, T)), D((2,)), D((2,)),
    ]

    def body(*refs):
        kernel(sections, T, *refs)

    routed = pl.pallas_call(
        body,
        out_shape=jax.ShapeDtypeStruct((2, rows, cols), BF16),
        in_specs=[pl.BlockSpec(memory_space=pl.ANY)] * 8,
        out_specs=pl.BlockSpec(memory_space=pltpu.VMEM),
        scratch_shapes=scratch,
        compiler_params=pltpu.CompilerParams(
            collective_id=0, has_side_effects=True, vmem_limit_bytes=50 * 1024 * 1024
        ),
        name="relay",
    )(acts, grads_in, head_grads, types, gains, w_query, w_key, w_value)
    return routed[None]


def solution(mesh):
    sections = mesh.shape["section"] // SUB

    def run(*args):
        return per_device(sections, *args)

    return jax.shard_map(
        run,
        mesh=mesh,
        in_specs=(
            P("section", None, None, "tensor"),
            P("section", None, None, "tensor"),
            P("section", None, None, "tensor"),
            P("section", None, None),
            P("section", None, None, None),
            P("section", None, None, "tensor"),
            P("section", None, None, "tensor"),
            P("section", None, None, "tensor"),
        ),
        out_specs=P("section", None, None, "tensor"),
        check_vma=False,
    )
```

time: 226 us -> 76.8 us (0.34)
  waiting for transfers between devices: 123 us -> 0 us
  Pallas kernels: 0 us -> 70.3 us
  blocking collectives: 54.3 us -> 0 us
  matrix products: 13.8 us -> 0 us
  between operations: 13.4 us -> 0.06 us
  other arithmetic: 9.83 us -> 0 us
  starting transfers between devices: 7.91 us -> 0 us
    ppermute x11 -> x0, waiting for transfers between devices: 78.9 us -> none  [the longest x10 75.4 us: swapped(): return lax.ppermute(value, axis, pairs)]
    pallas_call x0 -> x1, Pallas kernels: none -> 70.3 us  [per_device(): pl.pallas_call(body, out_shape=jax.ShapeDtypeStruct((2, rows, cols), BF16...]
    all_gather x3 -> x0, blocking collectives: 44.3 us -> none  [the longest x1 17.7 us: per_device(): x_cols = lax.all_gather(x_local, 'tensor', axis=2, tiled=True)]
    reduce_scatter x3 -> x0, waiting for transfers between devices: 43.8 us -> none  [the longest x2 29.9 us: sum_columns(): lax.psum_scatter(first, 'tensor', scatter_dimension=2, tiled=True)]
    dot_general x9 -> x0, matrix products: 13.8 us -> none  [the longest x1 5.55 us: per_device(): jnp.einsum('cth,cdh->ctd', joined_grads, joined_weights, preferred_elemen...]
    unnamed x1 -> x0, blocking collectives: 10 us -> none
    ppermute x11 -> x0, starting transfers between devices: 7.82 us -> none  [the longest x10 6.29 us: swapped(): return lax.ppermute(value, axis, pairs)]
    convert_element_type x5 -> x0, other arithmetic: 3.53 us -> none  [the longest x1 1.23 us: per_device(): result = (grad_local.astype(jnp.float32) + norm_grads).astype(jnp.bfloat16)]
  transfers between devices with their start and end apart: 14 -> 0, of which waited for: 11 -> 0; matrix products, arithmetic and copies ran while one was open for 4% -> 0% of each run, Pallas kernels for 0% -> 0%
where the time goes in v1:
time: 76.8 us; the launch traced here: 75.7 us
  Pallas kernels  70.3 us (92%)
  local copies, waits for them, and re-layouts  5.27 us (7%)
    pallas_call x1, Pallas kernels, per_device(): pl.pallas_call(body, out_shape=jax.ShapeDtypeStruct((2, rows, cols), BF16...  70.3 us
    unnamed x17, local copies, waits for them, and re-layouts  5.27 us

profile of v1, /device:TPU:0, one launch (start us, length us, event | category | flops | bytes accessed | tf_op | source)
XLA Modules:
  0.0 75.7 jit_solution(3755520424883634558)
XLA Ops:
  0.0 0.0 copy-start.6
  0.0 0.0 copy-start
  0.0 0.0 copy-start.1
  0.0 0.0 copy-start.2
  0.0 0.0 copy-start.3
  0.0 0.0 copy-start.4
  0.0 0.0 copy-start.5
  0.0 2.8 %copy.9 = bf16[1,2,4096,32]{3,2,1,0:T(8,128)(2,1)} copy(bf16[1,2,4096,32]{2,3,1,0:T(8,128)(2,1)} %param.14) | data formatting | bytes 1048576 | tf_op args[6]
  2.9 0.0 copy-done.6
  2.9 1.7 %copy.10 = bf16[1,2,4096,32]{3,2,1,0:T(8,128)(2,1)} copy(bf16[1,2,4096,32]{2,3,1,0:T(8,128)(2,1)S(1)} %copy-done.6) | data formatting | bytes 1048576 | tf_op args[7]
  4.6 0.0 copy-done
  4.6 0.0 copy-done.1
  4.6 0.0 copy-done.2
  4.6 0.0 copy-done.3
  4.6 0.0 copy-done.4
  4.7 0.0 copy-done.5
  4.7 70.3 %relay.1 = bf16[2,32,1024]{2,1,0:T(8,128)(2,1)S(1)} custom-call(bf16[2,32,1024]{2,1,0:T(8,128)(2,1)S(1)} %bitcast.11, bf16[2,32,1024]{2,1,0:T(8,128)(2,1)S(1)} %bitcast.12, bf16[2,128,128]{2,1,0:T(8,128)(2,1)S(1)} %bitcast.13, s32[2,32]{1,0:T(2,128)S(1)} %bitcast.15, bf16[2,2,1024]{2,1,0:T(2,128)(2,1)S(1)} %bitcast.14, bf16[2,4096,128]{2,1,0:T(8,128)(2,1)S(1)} %bitcast.9, ...), custom_call_target="tpu_custom_call" | custom-call | tf_op jit(solution)/shard_map/relay/pallas_call | solution.py:456
  75.0 0.7 copy.12
Async XLA Ops:
  0.0 2.9 %copy-start.6 = (bf16[1,2,4096,32]{2,3,1,0:T(8,128)(2,1)S(1)}, bf16[1,2,4096,32]{2,3,1,0:T(8,128)(2,1)}, u32[]{:S(2)}) copy-start(bf16[1,2,4096,32]{2,3,1,0:T(8,128)(2,1)} %param.15) | copy-start | bytes 1572868
  0.0 4.6 %copy-start = (bf16[1,2,4096,128]{3,2,1,0:T(8,128)(2,1)S(1)}, bf16[1,2,4096,128]{3,2,1,0:T(8,128)(2,1)}, u32[]{:S(2)}) copy-start(bf16[1,2,4096,128]{3,2,1,0:T(8,128)(2,1)} %param.13) | copy-start | bytes 6291460
  0.0 4.6 %copy-start.1 = (bf16[1,2,32,1024]{3,2,1,0:T(8,128)(2,1)S(1)}, bf16[1,2,32,1024]{3,2,1,0:T(8,128)(2,1)}, u32[]{:S(2)}) copy-start(bf16[1,2,32,1024]{3,2,1,0:T(8,128)(2,1)} %param.8) | copy-start | bytes 393220
  0.0 4.6 %copy-start.2 = (bf16[1,2,32,1024]{3,2,1,0:T(8,128)(2,1)S(1)}, bf16[1,2,32,1024]{3,2,1,0:T(8,128)(2,1)}, u32[]{:S(2)}) copy-start(bf16[1,2,32,1024]{3,2,1,0:T(8,128)(2,1)} %param.9) | copy-start | bytes 393220
  0.0 4.6 %copy-start.3 = (bf16[1,2,128,128]{3,2,1,0:T(8,128)(2,1)S(1)}, bf16[1,2,128,128]{3,2,1,0:T(8,128)(2,1)}, u32[]{:S(2)}) copy-start(bf16[1,2,128,128]{3,2,1,0:T(8,128)(2,1)} %param.10) | copy-start | bytes 196612
  0.0 4.6 %copy-start.4 = (bf16[1,2,2,1024]{3,2,1,0:T(2,128)(2,1)S(1)}, bf16[1,2,2,1024]{3,2,1,0:T(2,128)(2,1)}, u32[]{:S(2)}) copy-start(bf16[1,2,2,1024]{3,2,1,0:T(2,128)(2,1)} %param.12) | copy-start | bytes 24580
  0.0 4.6 %copy-start.5 = (s32[1,2,32]{2,1,0:T(2,128)S(1)}, s32[1,2,32]{2,1,0:T(2,128)}, u32[]{:S(2)}) copy-start(s32[1,2,32]{2,1,0:T(2,128)} %param.11) | copy-start | bytes 772

commit v2 on v1

--- a/solution.py
+++ b/solution.py
@@ -21,7 +21,7 @@
     sections, tensors,
     acts, grads, heads, types, gains, wq, wk, wv,
     out,
-    xg, kinds, gain_all, wqv, wkv, wvv, wcat, hg, gr, kindc, invc,
+    xg, kinds, gain_all, wqv, wkv, wvv, wcat, hg, gr, kindc, invc, acc, square,
     kvt, dkv, dkv_in, stat, stat_z, stat_s, stat_in,
     part, part_in, xs, xr, zs0, zr0, zs1, zr1, xs1, xr1, res,
     loc, ag_s, ag_r, small_s, small_r, kv_s, kv_r, dk_s, dk_r, st_s, st_r, sp_s, sp_r,
@@ -30,7 +30,7 @@
     spans, rows, cols = acts.shape
     n = SUB * rows
     hd = wq.shape[2]
-    kc = wk.shape[2]
+    kc = wk.shape[1]
     width = cols * tensors
     gcols = gains.shape[2]
     T = tensors
@@ -130,7 +130,26 @@
         for i in range(T):
             at = pl.ds(i * cols, cols)
             wcat[v, at, :hd] = wqv[v, at, :]
-            wcat[v, at, hd:] = jnp.concatenate([wkv[v, at, :], wvv[v, at, :]], axis=1)
+            kv_cols = jnp.concatenate([wkv[v, :, at], wvv[v, :, at]], axis=0)
+            wcat[v, at, hd:] = jnp.transpose(kv_cols)
+
+    acc[...] = jnp.zeros_like(acc)
+    square[...] = jnp.zeros_like(square)
+
+    def project(tt):
+        for p in (pos_pair, (1 - xi) * 2 + (1 - ci)):
+            for v in range(2):
+                ag_wait(v, p, tt)
+        block = tt * cols // gcols
+        off = pl.multiple_of(lax.rem(tt * cols, gcols), cols)
+        at = pl.ds(pl.multiple_of(tt * cols, cols), cols)
+        for v in range(2):
+            speech = kindc[v, :, 0:1] > 0.5
+            pair = gain_all[block, v, :, pl.ds(off, cols)].astype(F32)
+            xf = xg[v, :, at].astype(F32)
+            square[v] += jnp.broadcast_to(jnp.sum(xf * xf, axis=1, keepdims=True), (n, 128))
+            scaled = (xf * jnp.where(speech, pair[1:2, :], pair[0:1, :])).astype(BF16)
+            acc[v] += dot(scaled, wcat[v, at, :], ((1,), (0,)))
 
     join_weights(0)
 
@@ -138,102 +157,89 @@
     ag_sides(0, pos_x, t)
     ag_send(PAIR, 0, pos_x, t)
 
-    for k in range(1, T):
+    def each_side(k, action):
         for low in (True, False):
             tt = t - k if low else t + k
-            ok = tt >= 0 if low else tt < T
-            onward = t < T - 1 if low else t > 0
-            kind = RIGHT if low else LEFT
-
-            @pl.when(ok)
+
+            @pl.when(tt >= 0 if low else tt < T)
             def _():
-                ag_wait(1, pos, tt)
-
-                @pl.when(onward)
-                def _():
-                    ag_send(kind, 1, pos, tt)
-
-                ag_send(ACROSS, 1, pos, tt)
-                ag_send(PAIR, 1, pos, tt)
-                for p in (pos, pos_x):
-                    ag_wait(0, p, tt)
-
-                    @pl.when(onward)
-                    def _():
-                        ag_send(kind, 0, p, tt)
-
-                    ag_send(PAIR, 0, p, tt)
-
-        if k == 1:
-            join_weights(1)
-            ag_wait(1, pos_x, t)
-            ag_send(PAIR, 1, pos_x, t)
-    for k in range(1, T):
-        for low in (True, False):
-            tt = t - k if low else t + k
-            ok = tt >= 0 if low else tt < T
-
-            @pl.when(ok)
+                action(tt, low)
+
+    def forward(tt, low):
+        onward = t < T - 1 if low else t > 0
+        kind = RIGHT if low else LEFT
+        ag_wait(1, pos, tt)
+
+        @pl.when(onward)
+        def _():
+            ag_send(kind, 1, pos, tt)
+
+        ag_send(ACROSS, 1, pos, tt)
+        ag_send(PAIR, 1, pos, tt)
+        for p in (pos, pos_x):
+            ag_wait(0, p, tt)
+
+            @pl.when(onward)
             def _():
-                ag_wait(1, pos_x, tt)
-                ag_send(PAIR, 1, pos_x, tt)
-
-    for k in range(1, SUB):
-        source = lax.rem(pos - k + SUB, SUB)
-        arrived(kinds.at[source], small_r.at[0, k])
-        arrived(gain_all.at[source], small_r.at[1, k])
+                ag_send(kind, 0, p, tt)
+
+            ag_send(PAIR, 0, p, tt)
+
+    def share(tt):
+        ag_wait(1, pos_x, tt)
+        ag_send(PAIR, 1, pos_x, tt)
+
     eye_r = lax.broadcasted_iota(jnp.int32, (rows, rows), 0) == lax.broadcasted_iota(
         jnp.int32, (rows, rows), 1
     )
-    for v in range(2):
-        for p in range(SUB):
-            line = kinds[p, v : v + 1, :].astype(F32)
-            column = jnp.sum(jnp.where(eye_r, line, 0.0), axis=1, keepdims=True)
-            kindc[v, p * rows : (p + 1) * rows, :] = jnp.broadcast_to(column, (rows, 128))
-
-    for v in range(2):
-        for p in (pos_pair, (1 - xi) * 2 + (1 - ci)):
-            for tt in range(T):
-                ag_wait(v, p, tt)
+    for k in range(1, T):
+        each_side(k, forward)
+        if k == 1:
+            share(t)
+            join_weights(1)
+            for j in range(1, SUB):
+                source = lax.rem(pos - j + SUB, SUB)
+                arrived(kinds.at[source], small_r.at[0, j])
+                arrived(gain_all.at[source], small_r.at[1, j])
+            for v in range(2):
+                for p in range(SUB):
+                    line = kinds[p, v : v + 1, :].astype(F32)
+                    column = jnp.sum(jnp.where(eye_r, line, 0.0), axis=1, keepdims=True)
+                    kindc[v, p * rows : (p + 1) * rows, :] = jnp.broadcast_to(column, (rows, 128))
+            project(t)
+        else:
+            each_side(k - 1, lambda tt, low: share(tt))
+            each_side(k - 1, lambda tt, low: project(tt))
+    each_side(T - 1, lambda tt, low: share(tt))
+    each_side(T - 1, lambda tt, low: project(tt))
 
     hload.wait()
     eye = lax.broadcasted_iota(jnp.int32, (n, n), 0) == lax.broadcasted_iota(jnp.int32, (n, n), 1)
-    queries = []
-    for v in range(2):
-        speech = kindc[v, :, 0:1] > 0.5
-        total = jnp.zeros((n, hd + 2 * kc), F32)
-        square = jnp.zeros((n, 1), F32)
-        for i in range(T):
-            at = pl.ds(i * cols, cols)
-            block = i * cols // gcols
-            off = i * cols % gcols
-            pair = gain_all[block, v, :, off : off + cols].astype(F32)
-            xf = xg[v, :, at].astype(F32)
-            square = square + jnp.sum(xf * xf, axis=1, keepdims=True)
-            scaled = (xf * jnp.where(speech, pair[1:2, :], pair[0:1, :])).astype(BF16)
-            total = total + dot(scaled, wcat[v, at, :], ((1,), (0,)))
-        inverse = lax.rsqrt(square / width + EPS)
+    mine = pl.ds(pl.multiple_of(t * kc, kc), kc)
+    order = (1, 0)
+    queries = [None, None]
+    for v in order:
+        inverse = lax.rsqrt(square[v][:, 0:1] / width + EPS)
         invc[v] = jnp.broadcast_to(inverse, (n, 128))
-        total = total * inverse
-        queries.append(total[:, :hd].astype(BF16))
+        total = acc[v] * inverse
         turned = jnp.transpose(total[:, hd:]).astype(BF16)
-        mine = pl.ds(pl.multiple_of(t * kc, kc), kc)
         kvt[v, 0, mine, :] = turned[:kc]
         kvt[v, 1, mine, :] = turned[kc:]
-    mine = pl.ds(pl.multiple_of(t * kc, kc), kc)
-    for k in range(1, T):
-        send(kvt.at[:, :, mine, :], kvt.at[:, :, mine, :], kv_s.at[k], kv_r.at[k], z_peer(k))
-    for k in range(1, T):
-        source = lax.rem(t - k + T, T)
-        theirs = kvt.at[:, :, pl.ds(pl.multiple_of(source * kc, kc), kc), :]
-        arrived(theirs, kv_r.at[k])
+        for k in range(1, T):
+            block = kvt.at[v, :, mine, :]
+            send(block, block, kv_s.at[v, k], kv_r.at[v, k], z_peer(k))
+        queries[v] = total[:, :hd].astype(BF16)
 
     scale = hd ** (-0.5)
     causal = lax.broadcasted_iota(jnp.int32, (n, n), 0) >= lax.broadcasted_iota(
         jnp.int32, (n, n), 1
     )
-    query_grads = []
-    for v in range(2):
+    query_grads = [None, None]
+    for v in order:
+        for k in range(1, T):
+            source = lax.rem(t - k + T, T)
+            theirs = kvt.at[v, :, pl.ds(pl.multiple_of(source * kc, kc), kc), :]
+            arrived(theirs, kv_r.at[v, k])
         kt = kvt[v, 0]
         vt = kvt[v, 1]
         og = hg[v]
@@ -249,8 +255,11 @@
         value_each = dot(og, probs.astype(BF16), ((0,), (0,)))
         dkv[v, 0] = key_each.astype(BF16)
         dkv[v, 1] = value_each.astype(BF16)
+        for k in range(1, T):
+            goal = pl.ds(pl.multiple_of(lax.rem(t + k, T) * kc, kc), kc)
+            send(dkv.at[v, :, goal, :], dkv_in.at[k - 1, v], dk_s.at[v, k], dk_r.at[v, k], z_peer(k))
         qg = dot(sg, kt, ((1,), (1,)))
-        query_grads.append(qg.astype(BF16))
+        query_grads[v] = qg.astype(BF16)
         column = jnp.sum(qg * queries[v].astype(F32), axis=1, keepdims=True)
         line = jnp.sum(jnp.where(eye, column, 0.0), axis=0, keepdims=True)
         line = line + jnp.sum(
@@ -258,22 +267,75 @@
         )
         stat[v] = jnp.broadcast_to(line, (8, n))
     for k in range(1, T):
-        goal = pl.ds(pl.multiple_of(lax.rem(t + k, T) * kc, kc), kc)
-        send(dkv.at[:, :, goal, :], dkv_in.at[k - 1], dk_s.at[k], dk_r.at[k], z_peer(k))
         send(stat, stat_z.at[k - 1], st_s.at[k], st_r.at[k], z_peer(k))
-    summed = dkv[:, :, mine, :].astype(F32)
-    for k in range(1, T):
-        arrived(dkv_in.at[k - 1], dk_r.at[k])
-        summed = summed + dkv_in[k - 1].astype(F32)
-
-    for v in range(2):
-        kv_rows = jnp.transpose(summed[v].reshape(2 * kc, n)).astype(BF16)
+
+    goals = []
+    for i in range((T + 1) // 2):
+        goals += [T - 1 - i, i]
+    goals = goals[:T]
+
+    def terms(v, after_piece):
+        summed = dkv[v, :, mine, :].astype(F32)
+        for k in range(1, T):
+            arrived(dkv_in.at[k - 1, v], dk_r.at[v, k])
+            summed = summed + dkv_in[k - 1, v].astype(F32)
+        kv_rows = jnp.transpose(summed.reshape(2 * kc, n)).astype(BF16)
         joined = jnp.concatenate([query_grads[v], kv_rows], axis=1)
-        for i in range(T):
+        for j, i in enumerate(goals):
             piece = dot(joined, wcat[v, pl.ds(i * cols, cols), :], ((1,), (1,))).astype(BF16)
             for p in range(SUB):
                 part[v, p // 2, p % 2, i] = piece[p * rows : (p + 1) * rows]
             send(part.at[v, :, 1 - ci, i], part_in.at[v, :, i], pair_s.at[v, i], pair_r.at[v, i], pair_dev)
+            if j > 0:
+                after_piece(goals[j - 1])
+        after_piece(goals[-1])
+
+    def held0(i):
+        return (
+            part[0, xi, ci, i].astype(F32) + part_in[0, xi, i].astype(F32) + xr[i].astype(F32)
+        )
+
+    def held1(i):
+        return part[1, :, ci, i].astype(F32) + part_in[1, :, i].astype(F32)
+
+    bufs = ((zs0, zr0, held0), (zs1, zr1, held1))
+
+    def pass_on(v, goal, right):
+        stage, landing, held = bufs[v]
+        side = 0 if right else 1
+        dev = right_dev if right else left_dev
+        send(stage.at[goal], landing.at[side, goal], z_s.at[v, goal], z_r.at[v, side, goal], dev)
+
+    def begin(v, goal):
+        stage, landing, held = bufs[v]
+
+        @pl.when(jnp.logical_and(t == 0, goal > 0))
+        def _():
+            stage[goal] = held(goal).astype(BF16)
+            pass_on(v, goal, True)
+
+        @pl.when(jnp.logical_and(t == T - 1, goal < T - 1))
+        def _():
+            stage[goal] = held(goal).astype(BF16)
+            pass_on(v, goal, False)
+
+    def relay(v, goal, right):
+        stage, landing, held = bufs[v]
+        side = 0 if right else 1
+        arrived(landing.at[side, goal], z_r.at[v, side, goal])
+        stage[goal] = (held(goal) + landing[side, goal].astype(F32)).astype(BF16)
+        pass_on(v, goal, right)
+
+    def after_one(i):
+        arrived(part_in.at[1, :, i], pair_r.at[1, i])
+        begin(1, i)
+
+    def after_zero(i):
+        arrived(part_in.at[0, :, i], pair_r.at[0, i])
+        xs[i] = (part[0, 1 - xi, ci, i].astype(F32) + part_in[0, 1 - xi, i].astype(F32)).astype(BF16)
+        send(xs.at[i], xr.at[i], x_s.at[i], x_r.at[i], x_dev)
+
+    terms(1, after_one)
 
     line = stat[...]
     for k in range(1, T):
@@ -283,54 +345,26 @@
     for k in range(1, SUB):
         send(stat_s, stat_in.at[k - 1], sp_s.at[k], sp_r.at[k], pos_peer(k))
 
-    for i in range(T):
-        arrived(part_in.at[0, :, i], pair_r.at[0, i])
-        xs[i] = (part[0, 1 - xi, ci, i].astype(F32) + part_in[0, 1 - xi, i].astype(F32)).astype(BF16)
-        send(xs.at[i], xr.at[i], x_s.at[i], x_r.at[i], x_dev)
-    for i in range(T):
-        arrived(part_in.at[1, :, i], pair_r.at[1, i])
-
-    def held0(i):
-        return (
-            part[0, xi, ci, i].astype(F32) + part_in[0, xi, i].astype(F32) + xr[i].astype(F32)
-        )
-
-    def held1(i):
-        return part[1, :, ci, i].astype(F32) + part_in[1, :, i].astype(F32)
-
-    bufs = ((zs0, zr0, held0), (zs1, zr1, held1))
-
-    def step(v, goal, right):
-        stage, landing, held = bufs[v]
-        side = 0 if right else 1
-        first = t == 0 if right else t == T - 1
-        dev = right_dev if right else left_dev
-
-        @pl.when(first)
-        def _():
-            stage[goal] = held(goal).astype(BF16)
-
-        @pl.when(jnp.logical_not(first))
-        def _():
-            arrived(landing.at[side, goal], z_r.at[v, side, goal])
-            stage[goal] = (held(goal) + landing[side, goal].astype(F32)).astype(BF16)
-
-        send(stage.at[goal], landing.at[side, goal], z_s.at[v, goal], z_r.at[v, side, goal], dev)
+    terms(0, after_zero)
+
+    def relays(v, i):
+        high = T - 1 - i
+
+        @pl.when(jnp.logical_and(t > 0, t < high))
+        def _():
+            relay(v, high, True)
+
+        @pl.when(jnp.logical_and(t < T - 1, t > i))
+        def _():
+            relay(v, i, False)
 
     for i in range(T - 1):
-        for v in (1, 0):
-            if v == 0 and i == 0:
-                for j in range(T):
-                    arrived(xr.at[j], x_r.at[j])
-            high = T - 1 - i
-
-            @pl.when(t < high)
-            def _():
-                step(v, high, True)
-
-            @pl.when(t > i)
-            def _():
-                step(v, i, False)
+        relays(1, i)
+        if i == 0:
+            for goal in goals:
+                arrived(xr.at[goal], x_r.at[goal])
+                begin(0, goal)
+        relays(0, i)
 
     def settle(v):
         stage, landing, held = bufs[v]
@@ -403,9 +437,10 @@
         sent(gain_all.at[pos], small_s.at[1, k])
         sent(stat_s, sp_s.at[k])
     for k in range(1, T):
-        sent(kvt.at[:, :, mine, :], kv_s.at[k])
         goal = pl.ds(pl.multiple_of(lax.rem(t + k, T) * kc, kc), kc)
-        sent(dkv.at[:, :, goal, :], dk_s.at[k])
+        for v in range(2):
+            sent(kvt.at[v, :, mine, :], kv_s.at[v, k])
+            sent(dkv.at[v, :, goal, :], dk_s.at[v, k])
         sent(stat, st_s.at[k])
     for v in range(2):
         for i in range(T):
@@ -425,11 +460,11 @@
 def per_device(sections, acts, grads_in, head_grads, types, gains, w_query, w_key, w_value):
     T = lax.axis_size("tensor")
     acts, grads_in, head_grads, types, gains = acts[0], grads_in[0], head_grads[0], types[0], gains[0]
-    w_query, w_key, w_value = w_query[0], w_key[0], w_value[0]
+    w_query, w_key, w_value = w_query[0], jnp.swapaxes(w_key[0], 1, 2), jnp.swapaxes(w_value[0], 1, 2)
     spans, rows, cols = acts.shape
     n = SUB * rows
     hd = w_query.shape[2]
-    kc = w_key.shape[2]
+    kc = w_key.shape[1]
     width = cols * T
     V = pltpu.VMEM
     D = pltpu.SemaphoreType.DMA
@@ -437,7 +472,7 @@
         V((2, n, width), BF16), V((SUB, 2, rows), jnp.int32), V((SUB,) + gains.shape, BF16),
         V(w_query.shape, BF16), V(w_key.shape, BF16), V(w_value.shape, BF16),
         V((2, width, hd + 2 * kc), BF16), V(head_grads.shape, BF16), V(grads_in.shape, BF16),
-        V((2, n, 128), F32), V((2, n, 128), F32),
+        V((2, n, 128), F32), V((2, n, 128), F32), V((2, n, hd + 2 * kc), F32), V((2, n, 128), F32),
         V((2, 2, hd, n), BF16), V((2, 2, hd, n), BF16), V((T - 1, 2, 2, kc, n), BF16),
         V((2, 8, n), F32), V((T - 1, 2, 8, n), F32), V((2, 8, n), F32), V((SUB - 1, 2, 8, n), F32),
         V((2, 2, 2, T, rows, cols), BF16), V((2, 2, T, rows, cols), BF16),
@@ -446,7 +481,7 @@
         V((T, 2, rows, cols), BF16), V((2, T, 2, rows, cols), BF16),
         V((rows, cols), BF16), V((rows, cols), BF16), V((2, rows, cols), BF16),
         D((9,)), D((2, 4, SUB, T)), D((2, SUB, T)), D((2, SUB)), D((2, SUB)),
-        D((T,)), D((T,)), D((T,)), D((T,)), D((T,)), D((T,)), D((SUB,)), D((SUB,)),
+        D((2, T)), D((2, T)), D((2, T)), D((2, T)), D((T,)), D((T,)), D((SUB,)), D((SUB,)),
         D((2, T)), D((2, T)), D((T + 1,)), D((T + 1,)), D((2, T)), D((2, 2, T)), D((2,)), D((2,)),
     ]
 

time: 76.8 us -> 76.6 us (level)
  local copies, waits for them, and re-layouts: 5.27 us -> 8.35 us
  Pallas kernels: 70.3 us -> 67.3 us
    unnamed x17, local copies, waits for them, and re-layouts: 5.27 us -> 8.35 us
    pallas_call x1, Pallas kernels: 70.3 us -> 67.3 us  [per_device(): pl.pallas_call(body, out_shape=jax.ShapeDtypeStruct((2, rows, cols), BF16...]
where the time goes in v2:
time: 76.6 us; the launch traced here: 75.7 us
  Pallas kernels  67.3 us (88%)
  local copies, waits for them, and re-layouts  8.35 us (11%)
    pallas_call x1, Pallas kernels, per_device(): pl.pallas_call(body, out_shape=jax.ShapeDtypeStruct((2, rows, cols), BF16...  67.3 us
    unnamed x17, local copies, waits for them, and re-layouts  8.35 us

profile of v2, /device:TPU:0, one launch (start us, length us, event | category | flops | bytes accessed | tf_op | source)
XLA Modules:
  0.0 75.7 jit_solution(2038741634533516087)
XLA Ops:
  0.0 0.0 copy-start
  0.0 1.6 %copy-done = bf16[1,2,4096,128]{3,2,1,0:T(8,128)(2,1)S(1)} copy-done((bf16[1,2,4096,128]{3,2,1,0:T(8,128)(2,1)S(1)}, bf16[1,2,4096,128]{3,2,1,0:T(8,128)(2,1)}, u32[]{:S(2)}) %copy-start) | copy-done | bytes 2097176
  1.6 0.0 copy-start.1
  1.6 1.0 %copy-done.1 = bf16[1,2,4096,32]{2,3,1,0:T(8,128)(2,1)S(1)} copy-done((bf16[1,2,4096,32]{2,3,1,0:T(8,128)(2,1)S(1)}, bf16[1,2,4096,32]{2,3,1,0:T(8,128)(2,1)}, u32[]{:S(2)}) %copy-start.1) | copy-done | bytes 524312
  2.6 0.0 copy-start.2
  2.6 1.0 %copy-done.2 = bf16[1,2,4096,32]{2,3,1,0:T(8,128)(2,1)S(1)} copy-done((bf16[1,2,4096,32]{2,3,1,0:T(8,128)(2,1)S(1)}, bf16[1,2,4096,32]{2,3,1,0:T(8,128)(2,1)}, u32[]{:S(2)}) %copy-start.2) | copy-done | bytes 524312
  3.7 0.0 copy-start.3
  3.7 0.9 %copy-done.3 = bf16[1,2,32,1024]{3,2,1,0:T(8,128)(2,1)S(1)} copy-done((bf16[1,2,32,1024]{3,2,1,0:T(8,128)(2,1)S(1)}, bf16[1,2,32,1024]{3,2,1,0:T(8,128)(2,1)}, u32[]{:S(2)}) %copy-start.3) | copy-done | bytes 131096
  4.6 0.0 copy-start.4
  4.6 0.9 %copy-done.4 = bf16[1,2,32,1024]{3,2,1,0:T(8,128)(2,1)S(1)} copy-done((bf16[1,2,32,1024]{3,2,1,0:T(8,128)(2,1)S(1)}, bf16[1,2,32,1024]{3,2,1,0:T(8,128)(2,1)}, u32[]{:S(2)}) %copy-start.4) | copy-done | bytes 131096
  5.5 0.0 copy-start.5
  5.5 0.8 %copy-done.5 = bf16[1,2,128,128]{3,2,1,0:T(8,128)(2,1)S(1)} copy-done((bf16[1,2,128,128]{3,2,1,0:T(8,128)(2,1)S(1)}, bf16[1,2,128,128]{3,2,1,0:T(8,128)(2,1)}, u32[]{:S(2)}) %copy-start.5) | copy-done | bytes 65560
  6.3 0.0 copy-start.6
  6.3 0.7 copy-done.6
  7.0 0.0 copy-start.7
  7.0 0.7 copy-done.7
  7.7 67.3 %relay.1 = bf16[2,32,1024]{2,1,0:T(8,128)(2,1)S(1)} custom-call(bf16[2,32,1024]{2,1,0:T(8,128)(2,1)S(1)} %bitcast.17, bf16[2,32,1024]{2,1,0:T(8,128)(2,1)S(1)} %bitcast.18, bf16[2,128,128]{2,1,0:T(8,128)(2,1)S(1)} %bitcast.19, s32[2,32]{1,0:T(2,128)S(1)} %bitcast.21, bf16[2,2,1024]{2,1,0:T(2,128)(2,1)S(1)} %bitcast.20, bf16[2,4096,128]{2,1,0:T(8,128)(2,1)S(1)} %bitcast.13, ...), custom_call_target="tpu_custom_call" | custom-call | tf_op jit(solution)/shard_map/relay/pallas_call | solution.py:491
  75.0 0.7 copy.10
Async XLA Ops:
  0.0 1.6 %copy-start = (bf16[1,2,4096,128]{3,2,1,0:T(8,128)(2,1)S(1)}, bf16[1,2,4096,128]{3,2,1,0:T(8,128)(2,1)}, u32[]{:S(2)}) copy-start(bf16[1,2,4096,128]{3,2,1,0:T(8,128)(2,1)} %param.13) | copy-start | bytes 6291460
  1.6 1.0 %copy-start.1 = (bf16[1,2,4096,32]{2,3,1,0:T(8,128)(2,1)S(1)}, bf16[1,2,4096,32]{2,3,1,0:T(8,128)(2,1)}, u32[]{:S(2)}) copy-start(bf16[1,2,4096,32]{2,3,1,0:T(8,128)(2,1)} %param.14) | copy-start | bytes 1572868
  2.6 1.0 %copy-start.2 = (bf16[1,2,4096,32]{2,3,1,0:T(8,128)(2,1)S(1)}, bf16[1,2,4096,32]{2,3,1,0:T(8,128)(2,1)}, u32[]{:S(2)}) copy-start(bf16[1,2,4096,32]{2,3,1,0:T(8,128)(2,1)} %param.15) | copy-start | bytes 1572868
  3.7 0.9 %copy-start.3 = (bf16[1,2,32,1024]{3,2,1,0:T(8,128)(2,1)S(1)}, bf16[1,2,32,1024]{3,2,1,0:T(8,128)(2,1)}, u32[]{:S(2)}) copy-start(bf16[1,2,32,1024]{3,2,1,0:T(8,128)(2,1)} %param.8) | copy-start | bytes 393220
  4.6 0.9 %copy-start.4 = (bf16[1,2,32,1024]{3,2,1,0:T(8,128)(2,1)S(1)}, bf16[1,2,32,1024]{3,2,1,0:T(8,128)(2,1)}, u32[]{:S(2)}) copy-start(bf16[1,2,32,1024]{3,2,1,0:T(8,128)(2,1)} %param.9) | copy-start | bytes 393220
  5.5 0.8 %copy-start.5 = (bf16[1,2,128,128]{3,2,1,0:T(8,128)(2,1)S(1)}, bf16[1,2,128,128]{3,2,1,0:T(8,128)(2,1)}, u32[]{:S(2)}) copy-start(bf16[1,2,128,128]{3,2,1,0:T(8,128)(2,1)} %param.10) | copy-start | bytes 196612
  6.3 0.7 copy-start.6
  7.0 0.7 copy-start.7

commit v3 on v2

--- a/solution.py
+++ b/solution.py
@@ -23,7 +23,7 @@
     out,
     xg, kinds, gain_all, wqv, wkv, wvv, wcat, hg, gr, kindc, invc, acc, square,
     kvt, dkv, dkv_in, stat, stat_z, stat_s, stat_in,
-    part, part_in, xs, xr, zs0, zr0, zs1, zr1, xs1, xr1, res,
+    part, part_in, xs, xr, zs, zr, total, res,
     loc, ag_s, ag_r, small_s, small_r, kv_s, kv_r, dk_s, dk_r, st_s, st_r, sp_s, sp_r,
     pair_s, pair_r, x_s, x_r, z_s, z_r, route_s, route_r,
 ):
@@ -221,14 +221,14 @@
     for v in order:
         inverse = lax.rsqrt(square[v][:, 0:1] / width + EPS)
         invc[v] = jnp.broadcast_to(inverse, (n, 128))
-        total = acc[v] * inverse
-        turned = jnp.transpose(total[:, hd:]).astype(BF16)
+        projected = acc[v] * inverse
+        turned = jnp.transpose(projected[:, hd:]).astype(BF16)
         kvt[v, 0, mine, :] = turned[:kc]
         kvt[v, 1, mine, :] = turned[kc:]
         for k in range(1, T):
             block = kvt.at[v, :, mine, :]
             send(block, block, kv_s.at[v, k], kv_r.at[v, k], z_peer(k))
-        queries[v] = total[:, :hd].astype(BF16)
+        queries[v] = projected[:, :hd].astype(BF16)
 
     scale = hd ** (-0.5)
     causal = lax.broadcasted_iota(jnp.int32, (n, n), 0) >= lax.broadcasted_iota(
@@ -290,50 +290,46 @@
                 after_piece(goals[j - 1])
         after_piece(goals[-1])
 
-    def held0(i):
+    def held(v, i):
         return (
-            part[0, xi, ci, i].astype(F32) + part_in[0, xi, i].astype(F32) + xr[i].astype(F32)
+            part[v, xi, ci, i].astype(F32) + part_in[v, xi, i].astype(F32) + xr[v, i].astype(F32)
         )
 
-    def held1(i):
-        return part[1, :, ci, i].astype(F32) + part_in[1, :, i].astype(F32)
-
-    bufs = ((zs0, zr0, held0), (zs1, zr1, held1))
-
     def pass_on(v, goal, right):
-        stage, landing, held = bufs[v]
         side = 0 if right else 1
         dev = right_dev if right else left_dev
-        send(stage.at[goal], landing.at[side, goal], z_s.at[v, goal], z_r.at[v, side, goal], dev)
+        send(zs.at[v, goal], zr.at[v, side, goal], z_s.at[v, goal], z_r.at[v, side, goal], dev)
 
     def begin(v, goal):
-        stage, landing, held = bufs[v]
+        arrived(xr.at[v, goal], x_r.at[v, goal])
 
         @pl.when(jnp.logical_and(t == 0, goal > 0))
         def _():
-            stage[goal] = held(goal).astype(BF16)
+            zs[v, goal] = held(v, goal).astype(BF16)
             pass_on(v, goal, True)
 
         @pl.when(jnp.logical_and(t == T - 1, goal < T - 1))
         def _():
-            stage[goal] = held(goal).astype(BF16)
+            zs[v, goal] = held(v, goal).astype(BF16)
             pass_on(v, goal, False)
 
     def relay(v, goal, right):
-        stage, landing, held = bufs[v]
         side = 0 if right else 1
-        arrived(landing.at[side, goal], z_r.at[v, side, goal])
-        stage[goal] = (held(goal) + landing[side, goal].astype(F32)).astype(BF16)
+        arrived(zr.at[v, side, goal], z_r.at[v, side, goal])
+        zs[v, goal] = (held(v, goal) + zr[v, side, goal].astype(F32)).astype(BF16)
         pass_on(v, goal, right)
 
+    def cross(v, i):
+        arrived(part_in.at[v, :, i], pair_r.at[v, i])
+        xs[v, i] = (part[v, 1 - xi, ci, i].astype(F32) + part_in[v, 1 - xi, i].astype(F32)).astype(BF16)
+        send(xs.at[v, i], xr.at[v, i], x_s.at[v, i], x_r.at[v, i], x_dev)
+
     def after_one(i):
-        arrived(part_in.at[1, :, i], pair_r.at[1, i])
+        cross(1, i)
+
+    def after_zero(i):
+        cross(0, i)
         begin(1, i)
-
-    def after_zero(i):
-        arrived(part_in.at[0, :, i], pair_r.at[0, i])
-        xs[i] = (part[0, 1 - xi, ci, i].astype(F32) + part_in[0, 1 - xi, i].astype(F32)).astype(BF16)
-        send(xs.at[i], xr.at[i], x_s.at[i], x_r.at[i], x_dev)
 
     terms(1, after_one)
 
@@ -357,33 +353,6 @@
         @pl.when(jnp.logical_and(t < T - 1, t > i))
         def _():
             relay(v, i, False)
-
-    for i in range(T - 1):
-        relays(1, i)
-        if i == 0:
-            for goal in goals:
-                arrived(xr.at[goal], x_r.at[goal])
-                begin(0, goal)
-        relays(0, i)
-
-    def settle(v):
-        stage, landing, held = bufs[v]
-        stage[t] = held(t).astype(BF16)
-
-        @pl.when(t > 0)
-        def _():
-            arrived(landing.at[0, t], z_r.at[v, 0, t])
-            stage[t] = (stage[t].astype(F32) + landing[0, t].astype(F32)).astype(BF16)
-
-        @pl.when(t < T - 1)
-        def _():
-            arrived(landing.at[1, t], z_r.at[v, 1, t])
-            stage[t] = (stage[t].astype(F32) + landing[1, t].astype(F32)).astype(BF16)
-
-    settle(1)
-    xs1[...] = zs1[t, 1 - xi]
-    send(xs1, xr1, x_s.at[T], x_r.at[T], x_dev)
-    settle(0)
 
     grload.wait()
     line = stat_s[...]
@@ -396,7 +365,15 @@
     gain_block = t * cols // gcols
     gain_off = pl.multiple_of(lax.rem(t * cols, gcols), cols)
 
-    def finish(v, grad_sum):
+    def finish(v):
+        total[...] = held(v, t)
+        for side in range(2):
+
+            @pl.when(t > 0 if side == 0 else t < T - 1)
+            def _():
+                arrived(zr.at[v, side, t], z_r.at[v, side, t])
+                total[...] += zr[v, side, t].astype(F32)
+
         mean = jnp.sum(jnp.where(pick, line[v, 0:1, :], 0.0), axis=1, keepdims=True) / width
         inverse = invc[v, rowpos(pos), 0:1]
         speech = kindc[v, rowpos(pos), 0:1] > 0.5
@@ -404,14 +381,20 @@
         gain = jnp.where(speech, pair[1:2, :], pair[0:1, :])
         x = xg[v, rowpos(pos), pl.ds(pl.multiple_of(t * cols, cols), cols)].astype(F32)
         res[v] = (
-            gr[v].astype(F32) + inverse * gain * grad_sum - x * (inverse * inverse * mean)
+            gr[v].astype(F32) + inverse * gain * total[...] - x * (inverse * inverse * mean)
         ).astype(BF16)
         goal = jnp.where(here == 0, 1 - v, v)
         send(res.at[v], out.at[goal], route_s.at[v], route_r.at[goal], (before, t))
 
-    finish(0, zs0[t].astype(F32))
-    arrived(xr1, x_r.at[T])
-    finish(1, zs1[t, xi].astype(F32) + xr1[...].astype(F32))
+    for i in range(T - 1):
+        relays(1, i)
+    for i in goals:
+        begin(0, i)
+    relays(0, 0)
+    finish(1)
+    for i in range(1, T - 1):
+        relays(0, i)
+    finish(0)
 
     for v in range(2):
         for kind in (LEFT, RIGHT):
@@ -448,10 +431,8 @@
 
             @pl.when(i != t)
             def _():
-                sent(bufs[v][0].at[i], z_s.at[v, i])
-    for i in range(T):
-        sent(xs.at[i], x_s.at[i])
-    sent(xs1, x_s.at[T])
+                sent(zs.at[v, i], z_s.at[v, i])
+            sent(xs.at[v, i], x_s.at[v, i])
     for v in range(2):
         sent(res.at[v], route_s.at[v])
         arrived(out.at[v], route_r.at[v])
@@ -476,13 +457,12 @@
         V((2, 2, hd, n), BF16), V((2, 2, hd, n), BF16), V((T - 1, 2, 2, kc, n), BF16),
         V((2, 8, n), F32), V((T - 1, 2, 8, n), F32), V((2, 8, n), F32), V((SUB - 1, 2, 8, n), F32),
         V((2, 2, 2, T, rows, cols), BF16), V((2, 2, T, rows, cols), BF16),
-        V((T, rows, cols), BF16), V((T, rows, cols), BF16),
-        V((T, rows, cols), BF16), V((2, T, rows, cols), BF16),
-        V((T, 2, rows, cols), BF16), V((2, T, 2, rows, cols), BF16),
-        V((rows, cols), BF16), V((rows, cols), BF16), V((2, rows, cols), BF16),
+        V((2, T, rows, cols), BF16), V((2, T, rows, cols), BF16),
+        V((2, T, rows, cols), BF16), V((2, 2, T, rows, cols), BF16),
+        V((rows, cols), F32), V((2, rows, cols), BF16),
         D((9,)), D((2, 4, SUB, T)), D((2, SUB, T)), D((2, SUB)), D((2, SUB)),
         D((2, T)), D((2, T)), D((2, T)), D((2, T)), D((T,)), D((T,)), D((SUB,)), D((SUB,)),
-        D((2, T)), D((2, T)), D((T + 1,)), D((T + 1,)), D((2, T)), D((2, 2, T)), D((2,)), D((2,)),
+        D((2, T)), D((2, T)), D((2, T)), D((2, T)), D((2, T)), D((2, 2, T)), D((2,)), D((2,)),
     ]
 
     def body(*refs):

time: 76.6 us -> 75.9 us (level)
  no operation moved by 1% of the time
where the time goes in v3:
time: 75.9 us; the launch traced here: 75.5 us
  Pallas kernels  67.2 us (89%)
  local copies, waits for them, and re-layouts  8.35 us (11%)
    pallas_call x1, Pallas kernels, per_device(): pl.pallas_call(body, out_shape=jax.ShapeDtypeStruct((2, rows, cols), BF16...  67.2 us
    unnamed x17, local copies, waits for them, and re-layouts  8.35 us

profile of v3, /device:TPU:0, one launch (start us, length us, event | category | flops | bytes accessed | tf_op | source)
XLA Modules:
  0.0 75.5 jit_solution(1677334665238360823)
XLA Ops:
  0.0 0.0 copy-start
  0.0 1.6 %copy-done = bf16[1,2,4096,128]{3,2,1,0:T(8,128)(2,1)S(1)} copy-done((bf16[1,2,4096,128]{3,2,1,0:T(8,128)(2,1)S(1)}, bf16[1,2,4096,128]{3,2,1,0:T(8,128)(2,1)}, u32[]{:S(2)}) %copy-start) | copy-done | bytes 2097176
  1.6 0.0 copy-start.1
  1.6 1.0 %copy-done.1 = bf16[1,2,4096,32]{2,3,1,0:T(8,128)(2,1)S(1)} copy-done((bf16[1,2,4096,32]{2,3,1,0:T(8,128)(2,1)S(1)}, bf16[1,2,4096,32]{2,3,1,0:T(8,128)(2,1)}, u32[]{:S(2)}) %copy-start.1) | copy-done | bytes 524312
  2.6 0.0 copy-start.2
  2.6 1.0 %copy-done.2 = bf16[1,2,4096,32]{2,3,1,0:T(8,128)(2,1)S(1)} copy-done((bf16[1,2,4096,32]{2,3,1,0:T(8,128)(2,1)S(1)}, bf16[1,2,4096,32]{2,3,1,0:T(8,128)(2,1)}, u32[]{:S(2)}) %copy-start.2) | copy-done | bytes 524312
  3.7 0.0 copy-start.3
  3.7 0.9 %copy-done.3 = bf16[1,2,32,1024]{3,2,1,0:T(8,128)(2,1)S(1)} copy-done((bf16[1,2,32,1024]{3,2,1,0:T(8,128)(2,1)S(1)}, bf16[1,2,32,1024]{3,2,1,0:T(8,128)(2,1)}, u32[]{:S(2)}) %copy-start.3) | copy-done | bytes 131096
  4.6 0.0 copy-start.4
  4.6 0.9 %copy-done.4 = bf16[1,2,32,1024]{3,2,1,0:T(8,128)(2,1)S(1)} copy-done((bf16[1,2,32,1024]{3,2,1,0:T(8,128)(2,1)S(1)}, bf16[1,2,32,1024]{3,2,1,0:T(8,128)(2,1)}, u32[]{:S(2)}) %copy-start.4) | copy-done | bytes 131096
  5.5 0.0 copy-start.5
  5.5 0.8 %copy-done.5 = bf16[1,2,128,128]{3,2,1,0:T(8,128)(2,1)S(1)} copy-done((bf16[1,2,128,128]{3,2,1,0:T(8,128)(2,1)S(1)}, bf16[1,2,128,128]{3,2,1,0:T(8,128)(2,1)}, u32[]{:S(2)}) %copy-start.5) | copy-done | bytes 65560
  6.3 0.0 copy-start.6
  6.3 0.7 copy-done.6
  7.0 0.0 copy-start.7
  7.0 0.7 copy-done.7
  7.7 67.2 %relay.1 = bf16[2,32,1024]{2,1,0:T(8,128)(2,1)S(1)} custom-call(bf16[2,32,1024]{2,1,0:T(8,128)(2,1)S(1)} %bitcast.17, bf16[2,32,1024]{2,1,0:T(8,128)(2,1)S(1)} %bitcast.18, bf16[2,128,128]{2,1,0:T(8,128)(2,1)S(1)} %bitcast.19, s32[2,32]{1,0:T(2,128)S(1)} %bitcast.21, bf16[2,2,1024]{2,1,0:T(2,128)(2,1)S(1)} %bitcast.20, bf16[2,4096,128]{2,1,0:T(8,128)(2,1)S(1)} %bitcast.13, ...), custom_call_target="tpu_custom_call" | custom-call | tf_op jit(solution)/shard_map/relay/pallas_call | solution.py:471
  74.9 0.7 copy.10
Async XLA Ops:
  0.0 1.6 %copy-start = (bf16[1,2,4096,128]{3,2,1,0:T(8,128)(2,1)S(1)}, bf16[1,2,4096,128]{3,2,1,0:T(8,128)(2,1)}, u32[]{:S(2)}) copy-start(bf16[1,2,4096,128]{3,2,1,0:T(8,128)(2,1)} %param.13) | copy-start | bytes 6291460
  1.6 1.0 %copy-start.1 = (bf16[1,2,4096,32]{2,3,1,0:T(8,128)(2,1)S(1)}, bf16[1,2,4096,32]{2,3,1,0:T(8,128)(2,1)}, u32[]{:S(2)}) copy-start(bf16[1,2,4096,32]{2,3,1,0:T(8,128)(2,1)} %param.14) | copy-start | bytes 1572868
  2.6 1.0 %copy-start.2 = (bf16[1,2,4096,32]{2,3,1,0:T(8,128)(2,1)S(1)}, bf16[1,2,4096,32]{2,3,1,0:T(8,128)(2,1)}, u32[]{:S(2)}) copy-start(bf16[1,2,4096,32]{2,3,1,0:T(8,128)(2,1)} %param.15) | copy-start | bytes 1572868
  3.7 0.9 %copy-start.3 = (bf16[1,2,32,1024]{3,2,1,0:T(8,128)(2,1)S(1)}, bf16[1,2,32,1024]{3,2,1,0:T(8,128)(2,1)}, u32[]{:S(2)}) copy-start(bf16[1,2,32,1024]{3,2,1,0:T(8,128)(2,1)} %param.8) | copy-start | bytes 393220
  4.6 0.9 %copy-start.4 = (bf16[1,2,32,1024]{3,2,1,0:T(8,128)(2,1)S(1)}, bf16[1,2,32,1024]{3,2,1,0:T(8,128)(2,1)}, u32[]{:S(2)}) copy-start(bf16[1,2,32,1024]{3,2,1,0:T(8,128)(2,1)} %param.9) | copy-start | bytes 393220
  5.5 0.8 %copy-start.5 = (bf16[1,2,128,128]{3,2,1,0:T(8,128)(2,1)S(1)}, bf16[1,2,128,128]{3,2,1,0:T(8,128)(2,1)}, u32[]{:S(2)}) copy-start(bf16[1,2,128,128]{3,2,1,0:T(8,128)(2,1)} %param.10) | copy-start | bytes 196612
  6.3 0.7 copy-start.6
  7.0 0.7 copy-start.7

commit v4 on v3

--- a/solution.py
+++ b/solution.py
@@ -475,7 +475,7 @@
         out_specs=pl.BlockSpec(memory_space=pltpu.VMEM),
         scratch_shapes=scratch,
         compiler_params=pltpu.CompilerParams(
-            collective_id=0, has_side_effects=True, vmem_limit_bytes=50 * 1024 * 1024
+            collective_id=0, has_side_effects=True, vmem_limit_bytes=67_000_000
         ),
         name="relay",
     )(acts, grads_in, head_grads, types, gains, w_query, w_key, w_value)

time: 75.9 us -> 69 us (0.909)
  local copies, waits for them, and re-layouts: 8.35 us -> 1.57 us
    unnamed x17 -> x1, local copies, waits for them, and re-layouts: 8.35 us -> 1.57 us
where the time goes in v4:
time: 69 us; the launch traced here: 68.9 us
  Pallas kernels  67.3 us (98%)
  local copies, waits for them, and re-layouts  1.57 us (2%)
    pallas_call x1, Pallas kernels, per_device(): pl.pallas_call(body, out_shape=jax.ShapeDtypeStruct((2, rows, cols), BF16...  67.3 us
    unnamed x1, local copies, waits for them, and re-layouts  1.57 us

profile of v4, /device:TPU:0, one launch (start us, length us, event | category | flops | bytes accessed | tf_op | source)
XLA Modules:
  0.0 68.9 jit_solution(6843716397729313754)
XLA Ops:
  0.0 67.3 %relay.1 = bf16[2,32,1024]{2,1,0:T(8,128)(2,1)} custom-call(bf16[2,32,1024]{2,1,0:T(8,128)(2,1)} %bitcast.17, bf16[2,32,1024]{2,1,0:T(8,128)(2,1)} %bitcast.18, bf16[2,128,128]{2,1,0:T(8,128)(2,1)} %bitcast.19, s32[2,32]{1,0:T(2,128)} %bitcast.21, bf16[2,2,1024]{2,1,0:T(2,128)(2,1)} %bitcast.20, bf16[2,4096,128]{2,1,0:T(8,128)(2,1)} %bitcast.13, ...), custom_call_target="tpu_custom_call" | custom-call | tf_op jit(solution)/shard_map/relay/pallas_call | solution.py:471
  67.3 1.6 %copy.10 = bf16[1,2,32,1024]{3,2,1,0:T(8,128)(2,1)} copy(bf16[1,2,32,1024]{3,2,1,0:T(8,128)(2,1)} %bitcast.14) | data formatting | bytes 262144
